TPU v7x, 128 devices: a whole 4x4x4 slice. The times are simulated.
128 devices in a mesh: dp: 4 (over z), seq: 32 (over x, y, core).
Axes of the slice: x: 4, y: 4, z: 4, core: 2. Of those that a mesh axis runs over, the one named last changes fastest.
Arguments:
- queries: bfloat16 [4, 4096, 12288], P('dp', 'seq'), may hold values from -8 to 8
- keys_in: bfloat16 [4, 4096, 768], P('dp', 'seq'), may hold values from -8 to 8
- values_in: bfloat16 [4, 4096, 512], P('dp', 'seq'), may hold values from -6 to 6
- gate_cmp: float32 [4, 4096, 64], P('dp', 'seq'), may hold values from 0.05 to 0.95
- gate_win: float32 [4, 4096, 64], P('dp', 'seq'), may hold values from 0.05 to 0.95
- cotangent: bfloat16 [4, 4096, 8192], P('dp', 'seq'), may hold values from -6 to 6
- compress_key: bfloat16 [6144, 192], replicated, may hold values from -1 to 1
- compress_value: bfloat16 [4096, 128], replicated, may hold values from -0.09375 to 0.09375
Outputs:
- attended: bfloat16 [4, 4096, 8192], P('dp', 'seq')
- grad_query: bfloat16 [4, 4096, 12288], P('dp', 'seq')
- grad_key: bfloat16 [4, 4096, 768], P('dp', 'seq')
- grad_value: bfloat16 [4, 4096, 512], P('dp', 'seq')
- grad_gate_cmp: float32 [4, 4096, 64], P('dp', 'seq')
- grad_gate_win: float32 [4, 4096, 64], P('dp', 'seq')
- grad_compress_key: float32 [6144, 192], P('seq')
- grad_compress_value: float32 [4096, 128], P('seq')
All inputs are finite; a program needn't handle non-finite values.
Results may differ from a plain program's by a relative error of at most 0.023.
Values may be sent and summed in bfloat16 or wider, within the bound.
No kernel may reach another device: no remote copies, remote signals or barrier semaphores. Data moves between devices by JAX's collectives and lax.ppermute only.
A program may use at most 192 MiB of HBM per device.

v0:
```python
import functools
import functools
import math
import jax
import jax.numpy as jnp
from jax import lax
from jax.experimental import pallas as pl
from jax.experimental.pallas import tpu as pltpu
from jax.sharding import PartitionSpec as P


BLK = 32
STRIDE = 16
WIN = 512
NEG = -1e30
QB = 32


def stack_rows(ref, row, width, starts):
    parts = [ref[row : row + QB, at : at + width] for at in starts]
    return jnp.concatenate(parts, axis=0)


def nt(a, b):
    return lax.dot_general(a, b, (((1,), (1,)), ((), ())), preferred_element_type=jnp.float32)


def nn(a, b):
    return lax.dot_general(a, b, (((1,), (0,)), ((), ())), preferred_element_type=jnp.float32)


def lay_keys(pair, ke, ko, kt, rows, odd_group, dh):
    def even():
        lane = lax.broadcasted_iota(jnp.int32, (pair.shape[0], 256), 1)
        src = pair[:, :256].astype(jnp.float32)
        low = jnp.where(lane < dh, src, 0.0)
        ke[rows, :] = low.astype(jnp.bfloat16)
        ko[rows, :] = pltpu.roll(low, 256 - dh, 1).astype(jnp.bfloat16)
        kt[:, rows] = low.T[:dh].astype(jnp.bfloat16)

    def odd():
        lane = lax.broadcasted_iota(jnp.int32, (pair.shape[0], 256), 1)
        src = pair[:, 128:].astype(jnp.float32)
        high = jnp.where(lane >= 256 - dh, src, 0.0)
        low = pltpu.roll(high, dh, 1)
        ko[rows, :] = high.astype(jnp.bfloat16)
        ke[rows, :] = low.astype(jnp.bfloat16)
        kt[:, rows] = low.T[:dh].astype(jnp.bfloat16)

    pl.when(jnp.logical_not(odd_group))(even)
    pl.when(odd_group)(odd)


def join_keys_grad(acc_e, acc_o, scale, dh, odd_group, put):
    def even():
        lane = lax.broadcasted_iota(jnp.int32, acc_e.shape, 1)
        total = (acc_e[...] + pltpu.roll(acc_o[...], dh, 1)) * scale
        put(0, jnp.where(lane < dh, total, 0.0), False)

    def odd():
        lane = lax.broadcasted_iota(jnp.int32, acc_e.shape, 1)
        total = (acc_o[...] + pltpu.roll(acc_e[...], 256 - dh, 1)) * scale
        put(128, jnp.where(lane >= 256 - dh, total, 0.0), True)

    pl.when(jnp.logical_not(odd_group))(even)
    pl.when(odd_group)(odd)


def unit(qs, cs, gate, kx, vv, kt, vt, chunks, mask, valid, s_scr, g_scr, p_scr, u_scr, acc_k, acc_v, scale):
    to_log2 = scale * math.log2(math.e)
    first, last = chunks[0][0], chunks[-1][1]
    total = s_scr.shape[0]
    tops = []
    for at, end in chunks:
        s = mask(nt(kx[at:end, :], qs) * to_log2, at, end)
        s_scr[at:end, :] = s
        top = jnp.max(s, axis=0, keepdims=True)
        ok = valid(at)
        tops.append(top if ok is None else jnp.where(ok, top, NEG))
    top = tops[0]
    for other in tops[1:]:
        top = jnp.maximum(top, other)
    norm = jnp.zeros_like(top)
    mean = jnp.zeros_like(top)
    for at, end in chunks:
        ok = valid(at)
        base = top if ok is None else jnp.where(ok, top, -NEG)
        e = jnp.exp2(s_scr[at:end, :] - base)
        gp = nt(vv[at:end, :], cs)
        s_scr[at:end, :] = e
        g_scr[at:end, :] = gp
        norm = norm + jnp.sum(e, axis=0, keepdims=True)
        mean = mean + jnp.sum(e * gp, axis=0, keepdims=True)
    mean = mean / norm
    weight = gate / norm
    for at, end in chunks:
        p = s_scr[at:end, :] * weight
        u = (p * (g_scr[at:end, :] - mean)).astype(jnp.bfloat16)
        pb = p.astype(jnp.bfloat16)
        p_scr[at:end, :] = pb
        u_scr[at:end, :] = u
        acc_v[at:end, :] += nn(pb, cs)
        acc_k[at:end, :] += nn(u, qs)
    for lo, hi in ((0, first), (last, total)):
        if hi > lo:
            p_scr[lo:hi, :] = jnp.zeros((hi - lo, 256), jnp.bfloat16)
            u_scr[lo:hi, :] = jnp.zeros((hi - lo, 256), jnp.bfloat16)
    out = nn(vt[...], p_scr[...])
    dq = nn(kt[...], u_scr[...]) * scale
    return out, dq, mean


def cmp_kernel(first_ref, q_ref, c_ref, gate_ref, ck_ref, cv_ref, o_ref, dq_ref, gg_ref, gk_ref,
               ke, ko, kt, vt, s_e, s_o, g_e, g_o, p_e, p_o, u_e, u_o, acc_e, acc_o, acc_v, acc_w, *, dh, dv):
    group = pl.program_id(0)
    odd_group = group % 2 == 1
    scale = 1.0 / math.sqrt(dh)
    rows = ck_ref.shape[0]
    tokens = q_ref.shape[0]
    lay_keys(ck_ref, ke, ko, kt, slice(0, rows), odd_group, dh)
    vt[...] = cv_ref[...].astype(jnp.float32).T.astype(jnp.bfloat16)
    for acc in (acc_e, acc_o, acc_v, acc_w):
        acc[...] = jnp.zeros_like(acc)
    chunks = [(at, at + 128) for at in range(0, rows, 128)]
    heads = q_ref.shape[1] // dh // 2
    for block in range(tokens // QB):
        row = block * QB
        lane = lax.broadcasted_iota(jnp.int32, (1, 256), 1) & (QB - 1)
        limit = (first_ref[0] + row + 1 + lane) // STRIDE

        def mask(s, at, end):
            index = at + lax.broadcasted_iota(jnp.int32, (end - at, 256), 0)
            return jnp.where(index <= limit, s, NEG)

        for par, (kx, s, g, p, u, acc, accv) in enumerate(((ke, s_e, g_e, p_e, u_e, acc_e, acc_v), (ko, s_o, g_o, p_o, u_o, acc_o, acc_w))):
            qs = stack_rows(q_ref, row, 256, [2 * dh * h + par * 128 for h in range(heads)])
            cs = stack_rows(c_ref, row, dv, [(2 * h + par) * dv for h in range(heads)])
            at = 2 * block + par
            out, dq, mean = unit(qs, cs, gate_ref[0, at : at + 1, :], kx, cv_ref, kt, vt, chunks, mask,
                                 lambda at: None, s, g, p, u, acc, accv, scale)
            gg_ref[0, at : at + 1, :] = mean
            o_ref[0, at] = out.astype(jnp.bfloat16)
            dq_ref[0, block, par * dh : (par + 1) * dh, :] = dq.astype(jnp.bfloat16)
    base = pl.multiple_of((group // 2) * 2 * dh, 128)

    def put(at, value, add):
        if add:
            gk_ref[:, pl.ds(base + at, 128)] = (gk_ref[:, pl.ds(base + at, 128)].astype(jnp.float32) + value[:, :128]).astype(jnp.bfloat16)
            gk_ref[:, pl.ds(base + at + 128, 128)] = value[:, 128:].astype(jnp.bfloat16)
        else:
            gk_ref[:, pl.ds(base + at, 256)] = value.astype(jnp.bfloat16)

    join_keys_grad(acc_e, acc_o, scale, dh, odd_group, put)
    at = pl.multiple_of(4 * dh + group * dv, 128)
    gk_ref[:, pl.ds(at, dv)] = (acc_v[...] + acc_w[...]).astype(jnp.bfloat16)


def win_kernel(start_ref, q_ref, c_ref, gate_ref, k_ref, v_ref, h4, h3, h2, h1, oc_ref, dqc_ref, *refs, dh, dv, pair):
    refs = refs[2:] if pair else refs
    win_body(start_ref, q_ref, c_ref, gate_ref, k_ref, v_ref, (h4, h3, h2, h1), oc_ref, dqc_ref, *refs, dh=dh, dv=dv, pair=pair)


def win_body(start_ref, q_ref, c_ref, gate_ref, k_ref, v_ref, halo_refs, oc_ref, dqc_ref,
             o_ref, dq_ref, gg_ref, gh_ref, gown_ref,
               ke, ko, vv, kt, vt, s_e, s_o, g_e, g_o, p_e, p_o, u_e, u_o, acc_e, acc_o, acc_v, acc_w, *, dh, dv, pair):
    odd_group = pl.program_id(0) == 1
    scale = 1.0 / math.sqrt(dh)
    tokens = q_ref.shape[0]
    lead = WIN
    base = pair * 2 * dh
    vbase = pl.multiple_of(4 * dh + (2 * pair + pl.program_id(0)) * dv, 128)
    for n, h in enumerate(halo_refs):
        rows = slice(n * tokens, (n + 1) * tokens)
        lay_keys(h[:, pl.ds(base, 2 * dh)], ke, ko, kt, rows, odd_group, dh)
        vv[rows, :] = h[:, pl.ds(vbase, dv)]
    lay_keys(k_ref, ke, ko, kt, slice(lead, lead + tokens), odd_group, dh)
    vv[lead:, :] = v_ref[...]
    vt[...] = vv[...].astype(jnp.float32).T.astype(jnp.bfloat16)
    for acc in (acc_e, acc_o, acc_v, acc_w):
        acc[...] = jnp.zeros_like(acc)
    heads = q_ref.shape[1] // dh // 2

    def valid(at):
        return None if at >= lead else at >= start_ref[0]

    for block in range(tokens // QB):
        row = block * QB
        edges = sorted({row, row + QB, 128, 256, 384, 512, lead + row, lead + row + QB} - {0})
        edges = [row] + [x for x in edges if row < x <= lead + row + QB]
        chunks = list(zip(edges[:-1], edges[1:]))
        lane = lax.broadcasted_iota(jnp.int32, (QB, 256), 1) & (QB - 1)
        sub = lax.broadcasted_iota(jnp.int32, (QB, 256), 0)

        def mask(s, at, end):
            if at == row and end == row + QB:
                return jnp.where(sub > lane, s, NEG)
            if at == lead + row:
                return jnp.where(sub <= lane, s, NEG)
            return s

        dqs = []
        for par, (kx, s, g, p, u, acc, accv) in enumerate(((ke, s_e, g_e, p_e, u_e, acc_e, acc_v), (ko, s_o, g_o, p_o, u_o, acc_o, acc_w))):
            qs = stack_rows(q_ref, row, 256, [2 * dh * h + par * 128 for h in range(heads)])
            cs = stack_rows(c_ref, row, dv, [(2 * h + par) * dv for h in range(heads)])
            at = 2 * block + par
            out, dq, mean = unit(qs, cs, gate_ref[0, at : at + 1, :], kx, vv, kt, vt, chunks, mask,
                                 valid, s, g, p, u, acc, accv, scale)
            gg_ref[0, at : at + 1, :] = mean
            out = (out + oc_ref[0, at].astype(jnp.float32)).T
            for h in range(heads):
                o_ref[row : row + QB, (2 * h + par) * dv : (2 * h + par + 1) * dv] = out[h * QB : (h + 1) * QB].astype(jnp.bfloat16)
            dqs.append(dq + dqc_ref[0, block, par * dh : (par + 1) * dh, :].astype(jnp.float32))
        dq = jnp.concatenate(dqs, axis=0).T
        for h in range(heads):
            dq_ref[row : row + QB, 2 * dh * h : 2 * dh * (h + 1)] = dq[h * QB : (h + 1) * QB].astype(jnp.bfloat16)

    def put(at, value, add):
        for ref, lo, hi, kind in ((gh_ref, 0, lead, jnp.bfloat16), (gown_ref, lead, lead + tokens, jnp.float32)):
            part = value[lo:hi]
            if add:
                ref[:, at : at + 128] = (ref[:, at : at + 128].astype(jnp.float32) + part[:, :128]).astype(kind)
                ref[:, at + 128 : at + 256] = part[:, 128:].astype(kind)
            else:
                ref[:, at : at + 256] = part.astype(kind)

    join_keys_grad(acc_e, acc_o, scale, dh, odd_group, put)
    total = acc_v[...] + acc_w[...]
    vat = pl.multiple_of(2 * dh + pl.program_id(0) * dv, 128)
    gh_ref[:, pl.ds(vat, dv)] = total[:lead].astype(jnp.bfloat16)
    gown_ref[:, pl.ds(vat, dv)] = total[lead:]


def scratch(keys, dh, dv, own_values):
    f32, b16 = jnp.float32, jnp.bfloat16
    return [
        pltpu.VMEM((keys, 256), b16), pltpu.VMEM((keys, 256), b16),
        *([pltpu.VMEM((keys, dv), b16)] if own_values else []),
        pltpu.VMEM((dh, keys), b16), pltpu.VMEM((dv, keys), b16),
        *[pltpu.VMEM((keys, 256), f32)] * 4, *[pltpu.VMEM((keys, 256), b16)] * 4,
        pltpu.VMEM((keys, 256), f32), pltpu.VMEM((keys, 256), f32),
        pltpu.VMEM((keys, dv), f32), pltpu.VMEM((keys, dv), f32),
    ]


def attend_cmp(first, q, c, gate, ckv, groups, dh, dv):
    tokens, blocks = q.shape[0], ckv.shape[0]
    skip = groups * dh // dv
    wide, high = q.shape[1] // groups, c.shape[1] // groups
    steps = tokens // QB
    f32, b16 = jnp.float32, jnp.bfloat16
    return pl.pallas_call(
        functools.partial(cmp_kernel, dh=dh, dv=dv),
        grid=(groups,),
        in_specs=[
            pl.BlockSpec(memory_space=pltpu.SMEM),
            pl.BlockSpec((tokens, wide), lambda g: (0, g)),
            pl.BlockSpec((tokens, high), lambda g: (0, g)),
            pl.BlockSpec((1, 2 * steps, 256), lambda g: (g, 0, 0)),
            pl.BlockSpec((blocks, 2 * dh), lambda g: (0, g // 2)),
            pl.BlockSpec((blocks, dv), lambda g: (0, skip + g)),
        ],
        out_specs=[
            pl.BlockSpec((1, 2 * steps, dv, 256), lambda g: (g, 0, 0, 0)),
            pl.BlockSpec((1, steps, 2 * dh, 256), lambda g: (g, 0, 0, 0)),
            pl.BlockSpec((1, 2 * steps, 256), lambda g: (g, 0, 0)),
            pl.BlockSpec((blocks, groups * (dh + dv)), lambda g: (0, 0)),
        ],
        out_shape=[
            jax.ShapeDtypeStruct((groups, 2 * steps, dv, 256), b16),
            jax.ShapeDtypeStruct((groups, steps, 2 * dh, 256), b16),
            jax.ShapeDtypeStruct((groups, 2 * steps, 256), f32),
            jax.ShapeDtypeStruct((blocks, groups * (dh + dv)), b16),
        ],
        scratch_shapes=scratch(blocks, dh, dv, False),
        compiler_params=pltpu.CompilerParams(dimension_semantics=("arbitrary",), vmem_limit_bytes=56 * 2**20),
        cost_estimate=pl.CostEstimate(flops=blocks * tokens * 64 * 1920, transcendentals=blocks * tokens * 64, bytes_accessed=30_000_000),
        name="attend_cmp",
    )(first, q, c, gate, ckv, ckv)


def attend_win(start, q, c, gate, k, v, halos, oc, dqc, groups, dh, dv, pair, before):
    tokens = q.shape[0]
    wide, high = q.shape[1] // groups, c.shape[1] // groups
    steps = tokens // QB
    both = groups * (dh + dv)
    half = 2 * (dh + dv)
    f32, b16 = jnp.float32, jnp.bfloat16
    at = 2 * pair
    whole = lambda shape: pl.BlockSpec(shape, lambda g: (0,) * len(shape))
    return pl.pallas_call(
        functools.partial(win_kernel, dh=dh, dv=dv, pair=pair),
        grid=(2,),
        in_specs=[
            pl.BlockSpec(memory_space=pltpu.SMEM),
            pl.BlockSpec((tokens, wide), lambda g: (0, at + g)),
            pl.BlockSpec((tokens, high), lambda g: (0, at + g)),
            pl.BlockSpec((1, 2 * steps, 256), lambda g: (at + g, 0, 0)),
            pl.BlockSpec((tokens, 2 * dh), lambda g: (0, pair)),
            pl.BlockSpec((tokens, dv), lambda g: (0, at + g)),
            *[whole((tokens, both))] * 4,
            pl.BlockSpec((1, 2 * steps, dv, 256), lambda g: (at + g, 0, 0, 0)),
            pl.BlockSpec((1, steps, 2 * dh, 256), lambda g: (at + g, 0, 0, 0)),
            *[pl.BlockSpec(memory_space=pl.ANY)] * len(before),
        ],
        out_specs=[
            pl.BlockSpec((tokens, high), lambda g: (0, at + g)),
            pl.BlockSpec((tokens, wide), lambda g: (0, at + g)),
            pl.BlockSpec((1, 2 * steps, 256), lambda g: (g, 0, 0)),
            whole((WIN, half)),
            whole((tokens, half)),
        ],
        out_shape=[
            jax.ShapeDtypeStruct(c.shape, b16),
            jax.ShapeDtypeStruct(q.shape, b16),
            jax.ShapeDtypeStruct((2, 2 * steps, 256), f32),
            jax.ShapeDtypeStruct((WIN, half), b16),
            jax.ShapeDtypeStruct((tokens, half), f32),
        ],
        scratch_shapes=scratch(WIN + tokens, dh, dv, True),
        input_output_aliases={12: 0, 13: 1} if before else {},
        compiler_params=pltpu.CompilerParams(dimension_semantics=("arbitrary",), vmem_limit_bytes=56 * 2**20),
        cost_estimate=pl.CostEstimate(flops=320 * tokens * 64 * 1920, transcendentals=320 * tokens * 64, bytes_accessed=30_000_000),
        name="attend_win",
    )(start, q, c, gate, k, v, *halos, oc, dqc, *before)


def split_lanes(pair, dh, odd):
    lane = lax.broadcasted_iota(jnp.int32, (pair.shape[0], 256), 1)
    if odd:
        return jnp.where(lane >= 256 - dh, pair[:, 128:], 0.0)
    return jnp.where(lane < dh, pair[:, :256], 0.0)


def to_left(x, dh):
    return pltpu.roll(x, dh, 1)


def to_right(x, dh):
    return pltpu.roll(x, 256 - dh, 1)


def joined(left, right):
    return jnp.concatenate([left[:, :128], left[:, 128:] + right[:, :128], right[:, 128:]], axis=1)


def compress_kernel(k_ref, v_ref, prior_ref, wk_ref, wv_ref, out_ref, ext, y_scr, *, dh, dv, groups):
    tokens, kw = k_ref.shape
    tiles = ext.shape[0]
    for n in range(tiles):
        at = n * 128
        ext[n, :BLK, :] = prior_ref[:, at : at + 128].astype(jnp.float32)
        ref, at = (k_ref, at) if at < kw else (v_ref, at - kw)
        ext[n, BLK:, :] = ref[:, at : at + 128].astype(jnp.float32)

    def every(p):
        return jnp.concatenate([ext[n, pl.ds(p, blocks, stride=STRIDE), :] for n in range(tiles)], axis=1)

    blocks = tokens // STRIDE
    acc_k = jnp.zeros((groups * blocks, dh), jnp.float32)
    acc_v = jnp.zeros((groups * blocks, dv), jnp.float32)
    for p in range(0, BLK, 2):
        one, two = every(p), every(p + 1)
        rows = []
        for g in range(groups):
            at = (g // 2) * 2 * dh
            if g % 2 == 0:
                left = split_lanes(one[:, at : at + 2 * dh], dh, False)
                right = to_right(split_lanes(two[:, at : at + 2 * dh], dh, False), dh)
            else:
                left = to_left(split_lanes(one[:, at : at + 2 * dh], dh, True), dh)
                right = split_lanes(two[:, at : at + 2 * dh], dh, True)
            rows.append(joined(left, right))
        acc_k += nt(jnp.concatenate(rows, axis=0).astype(jnp.bfloat16), wk_ref[:, p * dh : (p + 2) * dh])
        vals = [
            jnp.concatenate([x[:, kw + g * dv : kw + (g + 1) * dv] for x in (one, two)], axis=1) for g in range(groups)
        ]
        acc_v += nn(jnp.concatenate(vals, axis=0).astype(jnp.bfloat16), wv_ref[p * dv : (p + 2) * dv, :])
    y_scr[...] = jnp.zeros_like(y_scr)
    y_scr[:, :dh] = acc_k
    for m in range(groups // 2):
        left = y_scr[2 * m * blocks : (2 * m + 1) * blocks, :]
        right = to_right(y_scr[(2 * m + 1) * blocks : (2 * m + 2) * blocks, :], dh)
        out_ref[:, 2 * m * dh : 2 * (m + 1) * dh] = joined(left, right).astype(jnp.bfloat16)
    for g in range(groups):
        out_ref[:, kw + g * dv : kw + (g + 1) * dv] = acc_v[g * blocks : (g + 1) * blocks].astype(jnp.bfloat16)


def compress(keys, values, prior, wk_t, wv, groups):
    dh, dv = wk_t.shape[0], wv.shape[1]
    blocks = keys.shape[0] // STRIDE
    both = keys.shape[1] + values.shape[1]
    return pl.pallas_call(
        functools.partial(compress_kernel, dh=dh, dv=dv, groups=groups),
        out_shape=jax.ShapeDtypeStruct((blocks, both), jnp.bfloat16),
        scratch_shapes=[
            pltpu.VMEM((both // 128, BLK + keys.shape[0], 128), jnp.float32),
            pltpu.VMEM((groups * blocks, 256), jnp.float32),
        ],
        compiler_params=pltpu.CompilerParams(vmem_limit_bytes=40 * 2**20),
        name="compress",
    )(keys, values, prior, wk_t, wv)


def back_kernel(shard_ref, grads_ref, rows_ref, wk_ref, wv_ref, part_ref, back_ref, wide, spread, *, dh, dv, groups):
    blocks, both = grads_ref.shape
    kw = groups * dh
    chunks = back_ref.shape[0] // STRIDE
    wide[:blocks, :] = grads_ref[...].astype(jnp.float32)
    wide[blocks:, :] = jnp.zeros((wide.shape[0] - blocks, both), jnp.float32)
    shard = shard_ref[0]
    lined = jnp.where(shard < STRIDE, wide[2 : blocks + 2, :], wide[1 : blocks + 1, :]).astype(jnp.bfloat16)
    flipped = rows_ref[...].astype(jnp.float32).T.astype(jnp.bfloat16)
    square = jnp.zeros((2 * dh, 2 * dh), jnp.float32)
    for m in range(groups // 2):
        at = 2 * m * dh
        square += nn(flipped[at : at + 2 * dh], lined[:, at : at + 2 * dh])
    low = square[:dh, :256] + to_left(split_lanes(square[dh:], dh, True), dh)
    part_v = jnp.zeros((dv, dv), jnp.float32)
    for g in range(groups):
        at = kw + g * dv
        part_v += nn(flipped[at : at + dv], lined[:, at : at + dv])
    part_ref[:, :256] = low.astype(jnp.bfloat16)
    part_ref[:dv, 256:] = part_v.astype(jnp.bfloat16)
    part_ref[dv:, 256:] = jnp.zeros((dh - dv, dv), jnp.bfloat16)
    here = wide[pl.ds(pl.multiple_of(shard * chunks, 8), chunks + 8), :]
    near, far = here[1 : chunks + 1], here[2 : chunks + 2]

    def stacked(x):
        rows = []
        for g in range(groups):
            half = split_lanes(x[:, (g // 2) * 2 * dh : (g // 2 + 1) * 2 * dh], dh, g % 2 == 1)
            rows.append(half if g % 2 == 0 else to_left(half, dh))
        return jnp.concatenate(rows, axis=0)[:, :dh].astype(jnp.bfloat16)

    far_k, near_k = stacked(far), stacked(near)
    vals = lambda x: jnp.concatenate([x[:, kw + g * dv : kw + (g + 1) * dv] for g in range(groups)], axis=0).astype(jnp.bfloat16)
    far_v, near_v = vals(far), vals(near)
    span = STRIDE * dh
    for p in range(0, STRIDE, 2):
        at = p * dh
        got = nn(far_k, wk_ref[:, at : at + 2 * dh]) + nn(near_k, wk_ref[:, span + at : span + at + 2 * dh])
        for m in range(groups // 2):
            a = got[2 * m * chunks : (2 * m + 1) * chunks]
            b = got[(2 * m + 1) * chunks : (2 * m + 2) * chunks]
            one = joined(split_lanes(a, dh, False), to_right(split_lanes(b, dh, False), dh))
            two = joined(to_left(split_lanes(a, dh, True), dh), split_lanes(b, dh, True))
            for n in range(3):
                lanes = slice(n * 128, n * 128 + 128)
                spread[3 * m + n, pl.ds(p, chunks, stride=STRIDE), :] = one[:, lanes]
                spread[3 * m + n, pl.ds(p + 1, chunks, stride=STRIDE), :] = two[:, lanes]
    for p in range(STRIDE):
        at = p * dv
        got = nt(far_v, wv_ref[at : at + dv, :]) + nt(near_v, wv_ref[STRIDE * dv + at : STRIDE * dv + at + dv, :])
        for g in range(groups):
            spread[kw // 128 + g, pl.ds(p, chunks, stride=STRIDE), :] = got[g * chunks : (g + 1) * chunks]
    for n in range(spread.shape[0]):
        back_ref[:, n * 128 : n * 128 + 128] = spread[n]


def compress_back(shard, grads, rows, wk_t, wv, tokens, groups):
    dh, dv = wk_t.shape[0], wv.shape[1]
    blocks, both = grads.shape
    vmem = pl.BlockSpec(memory_space=pltpu.VMEM)
    return pl.pallas_call(
        functools.partial(back_kernel, dh=dh, dv=dv, groups=groups),
        in_specs=[pl.BlockSpec(memory_space=pltpu.SMEM), vmem, vmem, vmem, vmem],
        out_shape=[
            jax.ShapeDtypeStruct((dh, 256 + dv), jnp.bfloat16),
            jax.ShapeDtypeStruct((tokens, both), jnp.float32),
        ],
        scratch_shapes=[
            pltpu.VMEM((blocks + 16, both), jnp.float32),
            pltpu.VMEM((both // 128, tokens, 128), jnp.float32),
        ],
        compiler_params=pltpu.CompilerParams(vmem_limit_bytes=40 * 2**20),
        name="compress_back",
    )(shard, grads, rows, wk_t, wv)


def gate_rows(gate, groups):
    tokens, heads = gate.shape
    cut = gate.reshape(tokens // QB, QB, groups, heads // groups // 2, 2)
    return cut.transpose(2, 0, 4, 3, 1).reshape(groups, 2 * (tokens // QB), -1)


def gate_columns(rows, tokens):
    groups = rows.shape[0]
    cut = rows.reshape(groups, tokens // QB, 2, -1, QB)
    return cut.transpose(1, 4, 0, 3, 2).reshape(tokens, -1)


def shifted(array, axis, by, wrap=False):
    devices = lax.axis_size(axis)
    if wrap:
        pairs = [(i, (i + by) % devices) for i in range(devices)]
    else:
        pairs = [(i, i + by) for i in range(devices) if 0 <= i + by < devices]
    return lax.ppermute(array, axis, pairs)


def to_sibling(array):
    return lax.ppermute(array, "seq", [(i, i ^ 1) for i in range(lax.axis_size("seq"))])


def between_chips(array):
    devices = lax.axis_size("seq")
    rings = [list(range(k, devices, 2)) for k in range(2)]
    return lax.all_to_all(array, "seq", 0, 0, axis_index_groups=rings, tiled=True)


def gathered(array, core):
    chips = lax.axis_size("seq") // 2
    mine = between_chips(jnp.broadcast_to(array[None], (chips, *array.shape)))
    other = to_sibling(mine)
    both = jnp.where(core == 0, jnp.stack([mine, other], axis=1), jnp.stack([other, mine], axis=1))
    return both.reshape(-1, array.shape[1])


def whole_step(queries, keys_in, values_in, gate_cmp, gate_win, cotangent, compress_key, compress_value):
    dh, dv = compress_key.shape[1], compress_value.shape[1]
    q, c, keys, values = queries[0], cotangent[0], keys_in[0], values_in[0]
    tokens, kw = keys.shape
    groups = kw // dh
    shard = lax.axis_index("seq").astype(jnp.int32).reshape(1)
    shards = lax.axis_size("seq")
    core = lax.axis_index("seq") % 2
    wk_t = compress_key.T
    last = jnp.concatenate([keys[tokens - BLK :], values[tokens - BLK :]], axis=1)
    prior = shifted(last, "seq", 1)
    own = jnp.concatenate([keys, values], axis=1)
    both = own.shape[1]
    cmp_own = compress(keys, values, prior, wk_t, compress_value, groups)
    cmp_all = gathered(cmp_own, core)
    held, _ = lax.optimization_barrier((own, cmp_own))
    two = shifted(held, "seq", 2)
    four = shifted(held, "seq", 4)
    one = to_sibling(jnp.where(core == 0, own, two))
    three = to_sibling(jnp.where(core == 0, two, four))
    halos = [four, three, two, one]
    first = shard * tokens
    start = jnp.maximum(WIN - first, 0)
    oc, dqc, ggc, gkc = attend_cmp(first, q, c, gate_rows(gate_cmp[0], groups), cmp_all, groups, dh, dv)
    mate = to_sibling(own)
    chip = jnp.where(core == 0, jnp.stack([own, mate]), jnp.stack([mate, own]))
    chip = chip.reshape(2 * tokens // STRIDE, STRIDE // 2, 2, both)
    residue = jnp.where(core == 0, chip[:, :, 0], chip[:, :, 1]).transpose(1, 0, 2)
    residue = jnp.concatenate([residue, residue], axis=0)
    gkc = gkc.reshape(shards // 2, 2, -1, both)
    blocks_dev = gkc.shape[2]
    folded = to_sibling(jnp.where(core == 0, gkc[:, 1], gkc[:, 0]))
    folded = folded.astype(jnp.float32) + jnp.where(core == 0, gkc[:, 0], gkc[:, 1]).astype(jnp.float32)
    sent = jnp.concatenate([folded.astype(jnp.bfloat16), residue], axis=1)
    got = between_chips(sent)
    gckb = jnp.sum(got[:, :blocks_dev].astype(jnp.float32), axis=0).astype(jnp.bfloat16)
    rows = got[:, blocks_dev:].reshape(-1, both)
    grads = gathered(gckb, core)
    win = functools.partial(attend_win, start, q, c, gate_rows(gate_win[0], groups), keys, values, halos, oc, dqc, groups, dh, dv)
    keeps, leads, ggw, out = [], [], [], ()
    for pair in range(groups // 2):
        *out, gg, gh, keep = win(pair, tuple(out))
        ggw.append(gg)
        leads.append(gh)
        keeps.append(keep)
    pieces = [jnp.concatenate([gh[n * tokens : (n + 1) * tokens] for gh in leads], axis=1) for n in range(4)]
    near, nearest = to_sibling(pieces[1]), to_sibling(pieces[3])
    near, nearest = near.astype(jnp.float32), nearest.astype(jnp.float32)
    to_two = (pieces[2].astype(jnp.float32) + jnp.where(core == 0, near, nearest)).astype(jnp.bfloat16)
    to_four = (pieces[0].astype(jnp.float32) + jnp.where(core == 0, 0.0, near)).astype(jnp.bfloat16)
    from_four, from_two = shifted(to_four, "seq", -4), shifted(to_two, "seq", -2)
    keep = jnp.concatenate(keeps, axis=1) + jnp.where(core == 0, nearest, 0.0)
    keep = keep + from_two.astype(jnp.float32) + from_four.astype(jnp.float32)
    half = 2 * (dh + dv)
    keys_back = jnp.concatenate([keep[:, at : at + 2 * dh] for at in (0, half)], axis=1)
    values_back = jnp.concatenate([keep[:, at + 2 * dh : at + half] for at in (0, half)], axis=1)
    attended, grad_query = out
    part, back = compress_back(shard, grads, rows, wk_t, compress_value, tokens, groups)
    parts = [shifted(part, "dp", by, True).astype(jnp.float32) for by in (1, 2, 3)]
    total = (part.astype(jnp.float32) + parts[1]) + (parts[0] + parts[2])
    grad_key = keys_back + back[:, :kw]
    grad_value = values_back + back[:, kw:]
    return (
        attended[None],
        grad_query[None],
        grad_key.astype(jnp.bfloat16)[None],
        grad_value.astype(jnp.bfloat16)[None],
        gate_columns(ggc, tokens)[None],
        gate_columns(jnp.concatenate(ggw, axis=0), tokens)[None],
        total[:, :dh],
        total[:dv, 256:],
    )


def solution(mesh):
    split, copied, rows = P("dp", "seq", None), P(), P("seq", None)
    return jax.shard_map(
        whole_step,
        mesh=mesh,
        in_specs=(split,) * 6 + (copied,) * 2,
        out_specs=(split,) * 6 + (rows,) * 2,
        check_vma=False,
    )
```

profile of v0, /device:TPU:1, one launch (start us, length us, event | category | flops | bytes accessed | tf_op | source)
XLA Modules:
  0.0 183.4 jit_solution(17343575475777622739)
XLA Ops:
  0.6 0.8 slice_bitcast_fusion.3
  1.4 0.8 slice_bitcast_fusion.2
  2.2 4.6 %collective-permute-start = (bf16[32,1280]{1,0:T(8,128)(2,1)S(1)}, bf16[32,1280]{1,0:T(8,128)(2,1)S(1)}, u32[]{:S(2)}, u32[]{:S(2)}) collective-permute-start(bf16[32,1280]{1,0:T(8,128)(2,1)S(1)} %pad_maximum_fusion.3), channel_id=1, source_target_pairs={{0,1},{1,2},{2,3},{3,4},{4,5},{5,6},{6,7},{7,8},{8,9},{9,10},{10,1... | collective-permute-start | bytes 245768 | tf_op jit(solution)/shard_map/ppermute | solution.py:498
  6.8 1.0 pad_maximum_fusion
  7.8 0.4 collective-permute-done.prior_ref
  8.3 1.7 copy-done
  9.9 1.2 copy-done.2
  11.2 0.9 copy-done.4
  12.1 0.9 copy-done.6
  13.0 1.4 compress.1
  14.4 3.2 %collective-permute-start.2 = (bf16[128,1280]{1,0:T(8,128)(2,1)S(1)}, bf16[128,1280]{1,0:T(8,128)(2,1)S(1)}, u32[]{:S(2)}, u32[]{:S(2)}) collective-permute-start(bf16[128,1280]{1,0:T(8,128)(2,1)S(1)} %pad_maximum_fusion), channel_id=1, source_target_pairs={{0,2},{1,3},{2,4},{3,5},{4,6},{5,7},{6,8},{7,9},{8,10},{9,11},{10,... | collective-permute-start | bytes 983048 | tf_op jit(solution)/shard_map/ppermute | solution.py:498
  17.6 4.1 %collective-permute-start.1 = (bf16[128,1280]{1,0:T(8,128)(2,1)S(1)}, bf16[128,1280]{1,0:T(8,128)(2,1)S(1)}, u32[]{:S(2)}, u32[]{:S(2)}) collective-permute-start(bf16[128,1280]{1,0:T(8,128)(2,1)S(1)} %pad_maximum_fusion), channel_id=1, source_target_pairs={{0,4},{1,5},{2,6},{3,7},{4,8},{5,9},{6,10},{7,11},{8,12},{9,13},{1... | collective-permute-start | bytes 983048 | tf_op jit(solution)/shard_map/ppermute | solution.py:498
  21.7 0.7 broadcast_in_dim.30
  22.5 5.7 %all-to-all-start = ((bf16[16,8,1280]{2,1,0:T(8,128)(2,1)}), bf16[16,8,1280]{2,1,0:T(8,128)(2,1)S(1)}, u32[]{:S(2)}, u32[]{:S(2)}) async-start(bf16[16,8,1280]{2,1,0:T(8,128)(2,1)} %broadcast_in_dim.30), calls=%async_computation | async-start | bytes 655360 | tf_op jit(solution)/shard_map/all_to_all | solution.py:508
  28.1 2.8 %collective-permute-start.11 = (bf16[128,1280]{1,0:T(8,128)(2,1)S(1)}, bf16[128,1280]{1,0:T(8,128)(2,1)S(1)}, u32[]{:S(2)}, u32[]{:S(2)}) collective-permute-start(bf16[128,1280]{1,0:T(8,128)(2,1)S(1)} %pad_maximum_fusion), channel_id=1, source_target_pairs={{0,1},{1,0},{2,3},{3,2},{4,5},{5,4},{6,7},{7,6},{8,9},{9,8},{10,11... | collective-permute-start | bytes 983048 | tf_op jit(solution)/shard_map/ppermute | solution.py:502
  31.1 0.7 reshape.66.gate_ref
  31.9 0.7 reshape.65.gate_ref
  32.7 4.3 %all-to-all-done = bf16[16,8,1280]{2,1,0:T(8,128)(2,1)S(1)} async-done(((bf16[16,8,1280]{2,1,0:T(8,128)(2,1)}), bf16[16,8,1280]{2,1,0:T(8,128)(2,1)S(1)}, u32[]{:S(2)}, u32[]{:S(2)}) %all-to-all-start) | async-done | bytes 327712 | tf_op jit(solution)/shard_map/all_to_all | solution.py:508
  37.0 4.8 %collective-permute-start.5 = (bf16[16,8,1280]{2,1,0:T(8,128)(2,1)S(1)}, bf16[16,8,1280]{2,1,0:T(8,128)(2,1)}, u32[]{:S(2)}, u32[]{:S(2)}) collective-permute-start(bf16[16,8,1280]{2,1,0:T(8,128)(2,1)S(1)} %all-to-all-done), channel_id=1, source_target_pairs={{0,1},{1,0},{2,3},{3,2},{4,5},{5,4},{6,7},{7,6},{8,9},{9,8},{10,11... | collective-permute-start | bytes 983048 | tf_op jit(solution)/shard_map/ppermute | solution.py:502
  41.9 0.1 fusion.13
  42.1 0.2 select_n.111
  42.4 0.2 copy-done.13
  42.6 0.1 copy-done.14
  42.7 0.5 collective-permute-start.3
  43.2 0.9 fusion.18
  44.1 0.4 fusion.9
  44.5 2.0 %maximum_select_fusion = bf16[16,2,8,1280]{3,2,1,0:T(8,128)(2,1)} fusion(bf16[16,1,8,1280]{3,2,1,0:T(8,128)(2,1)} %bitcast.11, bf16[16,1,8,1280]{3,2,1,0:T(8,128)(2,1)S(1)} %bitcast.84, pred[]{:T(512)S(6)} %eq.4), kind=kLoop, calls=%fused_computation.11 | loop fusion | flops 983040 | bytes 1310721 | tf_op jit(solution)/shard_map/jit(_where)/select_n | solution.py:515
  46.5 18.9 %attend_cmp.1 = (bf16[4,8,128,256]{3,2,1,0:T(8,128)(2,1)}, bf16[4,4,384,256]{3,2,1,0:T(8,128)(2,1)}, f32[4,8,256]{2,1,0:T(8,128)}, bf16[256,1280]{1,0:T(8,128)(2,1)}) custom-call(s32[1]{0:T(128)S(6)} %mul.3.first_ref, bf16[128,12288]{1,0:T(8,128)(2,1)} %bitcast.93, bf16[128,8192]{1,0:T(8,128)(2,1)} %bitcast.96, f32[4,8,256]{2,1,0:T(8,128)} %reshape.66.gate_ref, ...), custom_call_target="tpu_custom_call" | custom-call | flops 4026531840 | bytes 30000000 | tf_op jit(solution)/shard_map/attend_cmp/pallas_call | solution.py:251
  65.4 1.1 select_bitcast_fusion
  66.5 0.3 collective-permute-start.10
  66.8 0.7 copy-done.20
  67.5 0.1 copy-done.21
  67.6 20.9 %attend_win.2 = (bf16[128,8192]{1,0:T(8,128)(2,1)}, bf16[128,12288]{1,0:T(8,128)(2,1)}, f32[2,8,256]{2,1,0:T(8,128)}, bf16[512,640]{1,0:T(8,128)(2,1)}, f32[128,640]{1,0:T(8,128)}) custom-call(s32[1]{0:T(128)S(6)} %max.3.start_ref, bf16[128,12288]{1,0:T(8,128)(2,1)} %bitcast.94, bf16[128,8192]{1,0:T(8,128)(2,1)} %bitcast.97, f32[4,8,256]{2,1,0:T(8,128)} %reshape.65.gate_ref, ...), custom_call_target="tpu_custom_call" | custom-call | flops 5033164800 | bytes 30000000 | tf_op jit(solution)/shard_map/attend_win/pallas_call | solution.py:290
  88.6 21.2 %attend_win.3 = (bf16[128,8192]{1,0:T(8,128)(2,1)}, bf16[128,12288]{1,0:T(8,128)(2,1)}, f32[2,8,256]{2,1,0:T(8,128)}, bf16[512,640]{1,0:T(8,128)(2,1)}, f32[128,640]{1,0:T(8,128)}) custom-call(s32[1]{0:T(128)S(6)} %max.3.start_ref, bf16[128,12288]{1,0:T(8,128)(2,1)} %bitcast.95, ...), custom_call_target="tpu_custom_call", output_to_operand_aliasing={{0}: (12, {}), {1}: (13, {})} | custom-call | flops 5033164800 | bytes 30000000 | tf_op jit(solution)/shard_map/attend_win/pallas_call | solution.py:290
  109.8 1.3 fusion.16
  111.2 0.6 collective-permute-start.6
  111.9 0.1 fusion.7
  112.0 1.1 maximum_maximum_fusion
  113.1 3.8 %all-to-all-start.1 = ((bf16[16,24,1280]{2,1,0:T(8,128)(2,1)}), bf16[16,24,1280]{2,1,0:T(8,128)(2,1)S(1)}, u32[]{:S(2)}, u32[]{:S(2)}) async-start(bf16[16,24,1280]{2,1,0:T(8,128)(2,1)} %maximum_maximum_fusion), calls=%async_computation.1 | async-start | bytes 1966080 | tf_op jit(solution)/shard_map/all_to_all | solution.py:508
  116.9 0.9 fusion.4
  117.8 1.3 collective-permute-start.8
  119.1 1.3 collective-permute-start.9
  120.6 0.7 broadcast_in_dim_reshape.6
  121.5 0.7 broadcast_in_dim_reshape.7
  122.2 10.6 %all-to-all-done.1 = bf16[16,24,1280]{2,1,0:T(8,128)(2,1)S(1)} async-done(((bf16[16,24,1280]{2,1,0:T(8,128)(2,1)}), bf16[16,24,1280]{2,1,0:T(8,128)(2,1)S(1)}, u32[]{:S(2)}, u32[]{:S(2)}) %all-to-all-start.1) | async-done | bytes 983072 | tf_op jit(solution)/shard_map/all_to_all | solution.py:508
  132.9 0.9 broadcast_in_dim.34
  133.7 4.2 %all-to-all-start.2 = ((bf16[16,8,1280]{2,1,0:T(8,128)(2,1)}), bf16[16,8,1280]{2,1,0:T(8,128)(2,1)}, u32[]{:S(2)}, u32[]{:S(2)}) async-start(bf16[16,8,1280]{2,1,0:T(8,128)(2,1)} %broadcast_in_dim.34), calls=%async_computation.2 | async-start | bytes 655360 | tf_op jit(solution)/shard_map/all_to_all | solution.py:508
  137.9 6.1 %collective-permute-done.8 = bf16[128,1280]{1,0:T(8,128)(2,1)S(1)} collective-permute-done((bf16[128,1280]{1,0:T(8,128)(2,1)}, bf16[128,1280]{1,0:T(8,128)(2,1)S(1)}, u32[]{:S(2)}, u32[]{:S(2)}) %collective-permute-start.8) | collective-permute-done | bytes 327712 | tf_op jit(solution)/shard_map/ppermute | solution.py:498
  144.0 1.0 fusion.2
  145.0 7.3 %all-to-all-done.2 = bf16[16,8,1280]{2,1,0:T(8,128)(2,1)} async-done(((bf16[16,8,1280]{2,1,0:T(8,128)(2,1)}), bf16[16,8,1280]{2,1,0:T(8,128)(2,1)}, u32[]{:S(2)}, u32[]{:S(2)}) %all-to-all-start.2) | async-done | bytes 327712 | tf_op jit(solution)/shard_map/all_to_all | solution.py:508
  152.4 10.2 %collective-permute-start.12 = (bf16[16,8,1280]{2,1,0:T(8,128)(2,1)}, bf16[16,8,1280]{2,1,0:T(8,128)(2,1)S(1)}, u32[]{:S(2)}, u32[]{:S(2)}) collective-permute-start(bf16[16,8,1280]{2,1,0:T(8,128)(2,1)} %all-to-all-done.2), channel_id=1, source_target_pairs={{0,1},{1,0},{2,3},{3,2},{4,5},{5,4},{6,7},{7,6},{8,9},{9,8},{10,11... | collective-permute-start | bytes 983048 | tf_op jit(solution)/shard_map/ppermute | solution.py:502
  162.5 1.0 fusion.14
  163.5 1.1 fusion.15
  164.6 1.1 slice.113
  165.7 1.2 maximum_select_fusion.2
  166.9 1.7 compress_back.1
  168.6 3.8 %collective-permute-start.15 = (bf16[192,384]{1,0:T(8,128)(2,1)S(1)}, bf16[192,384]{1,0:T(8,128)(2,1)S(1)}, u32[]{:S(2)}, u32[]{:S(2)}) collective-permute-start(bf16[192,384]{1,0:T(8,128)(2,1)S(1)} %get-tuple-element.41), channel_id=1, source_target_pairs={{0,96},{32,0},{64,32},{96,64},{1,97},{33,1},{65,33},{97,65},{2,98}... | collective-permute-start | bytes 442376 | tf_op jit(solution)/shard_map/ppermute | solution.py:498
  172.5 1.3 collective-permute-start.13
  173.8 0.7 fusion.11
  174.5 0.7 fusion.12
  175.2 0.5 collective-permute-done.15
  175.7 6.3 %collective-permute-done.14 = bf16[192,384]{1,0:T(8,128)(2,1)S(1)} collective-permute-done((bf16[192,384]{1,0:T(8,128)(2,1)S(1)}, bf16[192,384]{1,0:T(8,128)(2,1)S(1)}, u32[]{:S(2)}, u32[]{:S(2)}) %collective-permute-start.14) | collective-permute-done | bytes 147488 | tf_op jit(solution)/shard_map/ppermute | solution.py:498
  182.0 0.6 slice.117
  182.7 0.7 slice.116
  (66 shorter events, 1.0 us)
Async XLA Ops:
  2.2 6.1 %collective-permute-start = (bf16[32,1280]{1,0:T(8,128)(2,1)S(1)}, bf16[32,1280]{1,0:T(8,128)(2,1)S(1)}, u32[]{:S(2)}, u32[]{:S(2)}) collective-permute-start(bf16[32,1280]{1,0:T(8,128)(2,1)S(1)} %pad_maximum_fusion.3), channel_id=1, source_target_pairs={{0,1},{1,2},{2,3},{3,4},{4,5},{5,6},{6,7},{7,8},{8,9},{9,10},{10,1... | collective-permute-start | bytes 245768 | tf_op jit(solution)/shard_map/ppermute | solution.py:498
  8.3 1.7 copy-start
  9.9 1.2 copy-start.2
  11.2 0.9 copy-start.4
  12.1 0.9 copy-start.6
  13.0 17.9 %copy-start.15 = (f32[1,128,64]{1,2,0:T(8,128)S(1)}, f32[1,128,64]{1,2,0:T(8,128)}, u32[]{:S(2)}) copy-start(f32[1,128,64]{1,2,0:T(8,128)} %param.11) | copy-start | bytes 98308
  13.0 18.8 %copy-start.16 = (f32[1,128,64]{1,2,0:T(8,128)S(1)}, f32[1,128,64]{1,2,0:T(8,128)}, u32[]{:S(2)}) copy-start(f32[1,128,64]{1,2,0:T(8,128)} %param.12) | copy-start | bytes 98308
  13.0 28.8 %copy-start.5 = (bf16[1,128,768]{2,1,0:T(8,128)(2,1)S(1)}, bf16[1,128,768]{2,1,0:T(8,128)(2,1)}, u32[]{:S(2)}) copy-start(bf16[1,128,768]{2,1,0:T(8,128)(2,1)} %param.9) | copy-start | bytes 589828
  13.0 28.8 %copy-start.7 = (bf16[1,128,512]{2,1,0:T(8,128)(2,1)S(1)}, bf16[1,128,512]{2,1,0:T(8,128)(2,1)}, u32[]{:S(2)}) copy-start(bf16[1,128,512]{2,1,0:T(8,128)(2,1)} %param.10) | copy-start | bytes 393220
  14.4 27.4 %collective-permute-start.2 = (bf16[128,1280]{1,0:T(8,128)(2,1)S(1)}, bf16[128,1280]{1,0:T(8,128)(2,1)S(1)}, u32[]{:S(2)}, u32[]{:S(2)}) collective-permute-start(bf16[128,1280]{1,0:T(8,128)(2,1)S(1)} %pad_maximum_fusion), channel_id=1, source_target_pairs={{0,2},{1,3},{2,4},{3,5},{4,6},{5,7},{6,8},{7,9},{8,10},{9,11},{10,... | collective-permute-start | bytes 983048 | tf_op jit(solution)/shard_map/ppermute | solution.py:498
  17.6 24.2 %collective-permute-start.1 = (bf16[128,1280]{1,0:T(8,128)(2,1)S(1)}, bf16[128,1280]{1,0:T(8,128)(2,1)S(1)}, u32[]{:S(2)}, u32[]{:S(2)}) collective-permute-start(bf16[128,1280]{1,0:T(8,128)(2,1)S(1)} %pad_maximum_fusion), channel_id=1, source_target_pairs={{0,4},{1,5},{2,6},{3,7},{4,8},{5,9},{6,10},{7,11},{8,12},{9,13},{1... | collective-permute-start | bytes 983048 | tf_op jit(solution)/shard_map/ppermute | solution.py:498
  22.5 14.5 %all-to-all-start = ((bf16[16,8,1280]{2,1,0:T(8,128)(2,1)}), bf16[16,8,1280]{2,1,0:T(8,128)(2,1)S(1)}, u32[]{:S(2)}, u32[]{:S(2)}) async-start(bf16[16,8,1280]{2,1,0:T(8,128)(2,1)} %broadcast_in_dim.30), calls=%async_computation | async-start | bytes 655360 | tf_op jit(solution)/shard_map/all_to_all | solution.py:508
  28.1 13.9 %collective-permute-start.11 = (bf16[128,1280]{1,0:T(8,128)(2,1)S(1)}, bf16[128,1280]{1,0:T(8,128)(2,1)S(1)}, u32[]{:S(2)}, u32[]{:S(2)}) collective-permute-start(bf16[128,1280]{1,0:T(8,128)(2,1)S(1)} %pad_maximum_fusion), channel_id=1, source_target_pairs={{0,1},{1,0},{2,3},{3,2},{4,5},{5,4},{6,7},{7,6},{8,9},{9,8},{10,11... | collective-permute-start | bytes 983048 | tf_op jit(solution)/shard_map/ppermute | solution.py:502
  37.0 7.5 %collective-permute-start.5 = (bf16[16,8,1280]{2,1,0:T(8,128)(2,1)S(1)}, bf16[16,8,1280]{2,1,0:T(8,128)(2,1)}, u32[]{:S(2)}, u32[]{:S(2)}) collective-permute-start(bf16[16,8,1280]{2,1,0:T(8,128)(2,1)S(1)} %all-to-all-done), channel_id=1, source_target_pairs={{0,1},{1,0},{2,3},{3,2},{4,5},{5,4},{6,7},{7,6},{8,9},{9,8},{10,11... | collective-permute-start | bytes 983048 | tf_op jit(solution)/shard_map/ppermute | solution.py:502
  41.8 0.8 copy-start.13
  41.8 0.9 copy-start.14
  42.7 24.1 %collective-permute-start.4 = (bf16[128,1280]{1,0:T(8,128)(2,1)S(1)}, bf16[128,1280]{1,0:T(8,128)(2,1)S(1)}, u32[]{:S(2)}, u32[]{:S(2)}) collective-permute-start(bf16[128,1280]{1,0:T(8,128)(2,1)S(1)} %get-tuple-element.59), channel_id=1, source_target_pairs={{0,1},{1,0},{2,3},{3,2},{4,5},{5,4},{6,7},{7,6},{8,9},{9,8},{10,11... | collective-permute-start | bytes 983048 | tf_op jit(solution)/shard_map/ppermute | solution.py:502
  42.7 24.1 %collective-permute-start.3 = (bf16[128,1280]{1,0:T(8,128)(2,1)S(1)}, bf16[128,1280]{1,0:T(8,128)(2,1)S(1)}, u32[]{:S(2)}, u32[]{:S(2)}) collective-permute-start(bf16[128,1280]{1,0:T(8,128)(2,1)S(1)} %get-tuple-element.60), channel_id=1, source_target_pairs={{0,1},{1,0},{2,3},{3,2},{4,5},{5,4},{6,7},{7,6},{8,9},{9,8},{10,11... | collective-permute-start | bytes 983048 | tf_op jit(solution)/shard_map/ppermute | solution.py:502
  66.5 45.4 %collective-permute-start.10 = (bf16[16,8,1280]{2,1,0:T(8,128)(2,1)S(1)}, bf16[16,8,1280]{2,1,0:T(8,128)(2,1)S(1)}, u32[]{:S(2)}, u32[]{:S(2)}) collective-permute-start(bf16[16,8,1280]{2,1,0:T(8,128)(2,1)S(1)} %select_bitcast_fusion), channel_id=1, source_target_pairs={{0,1},{1,0},{2,3},{3,2},{4,5},{5,4},{6,7},{7,6},{8,9},{9,8},{10,11... | collective-permute-start | bytes 983048 | tf_op jit(solution)/shard_map/ppermute | solution.py:502
  66.8 0.7 copy-start.20
  66.8 0.8 copy-start.21
  88.6 21.2 %copy-start.10 = (bf16[512,640]{1,0:T(8,128)(2,1)S(1)}, bf16[512,640]{1,0:T(8,128)(2,1)}, u32[]{:S(2)}) copy-start(bf16[512,640]{1,0:T(8,128)(2,1)} %get-tuple-element.34) | copy-start | bytes 1966084
  109.8 2.1 %copy-start.9 = (bf16[256,1280]{1,0:T(8,128)(2,1)S(1)}, bf16[256,1280]{1,0:T(8,128)(2,1)}, u32[]{:S(2)}) copy-start(bf16[256,1280]{1,0:T(8,128)(2,1)} %get-tuple-element.36) | copy-start | bytes 1966084
  111.2 5.7 %collective-permute-start.6 = (bf16[128,1280]{1,0:T(8,128)(2,1)S(1)}, bf16[128,1280]{1,0:T(8,128)(2,1)S(1)}, u32[]{:S(2)}, u32[]{:S(2)}) collective-permute-start(bf16[128,1280]{1,0:T(8,128)(2,1)S(1)} %pad_maximum_fusion.1), channel_id=1, source_target_pairs={{0,1},{1,0},{2,3},{3,2},{4,5},{5,4},{6,7},{7,6},{8,9},{9,8},{10,11... | collective-permute-start | bytes 983048 | tf_op jit(solution)/shard_map/ppermute | solution.py:502
  111.8 5.1 %collective-permute-start.7 = (bf16[128,1280]{1,0:T(8,128)(2,1)S(1)}, bf16[128,1280]{1,0:T(8,128)(2,1)S(1)}, u32[]{:S(2)}, u32[]{:S(2)}) collective-permute-start(bf16[128,1280]{1,0:T(8,128)(2,1)S(1)} %pad_maximum_fusion.2), channel_id=1, source_target_pairs={{0,1},{1,0},{2,3},{3,2},{4,5},{5,4},{6,7},{7,6},{8,9},{9,8},{10,11... | collective-permute-start | bytes 983048 | tf_op jit(solution)/shard_map/ppermute | solution.py:502
  113.1 7.3 %copy-start.17 = (f32[4,8,256]{2,1,0:T(8,128)S(1)}, f32[4,8,256]{2,1,0:T(8,128)}, u32[]{:S(2)}) copy-start(f32[4,8,256]{2,1,0:T(8,128)} %get-tuple-element.38) | copy-start | bytes 98308
  113.1 8.2 %copy-start.18 = (f32[2,8,256]{2,1,0:T(8,128)S(1)}, f32[2,8,256]{2,1,0:T(8,128)}, u32[]{:S(2)}) copy-start(f32[2,8,256]{2,1,0:T(8,128)} %get-tuple-element.39) | copy-start | bytes 49156
  113.1 8.2 %copy-start.19 = (f32[2,8,256]{2,1,0:T(8,128)S(1)}, f32[2,8,256]{2,1,0:T(8,128)}, u32[]{:S(2)}) copy-start(f32[2,8,256]{2,1,0:T(8,128)} %get-tuple-element.40) | copy-start | bytes 49156
  113.1 19.7 %all-to-all-start.1 = ((bf16[16,24,1280]{2,1,0:T(8,128)(2,1)}), bf16[16,24,1280]{2,1,0:T(8,128)(2,1)S(1)}, u32[]{:S(2)}, u32[]{:S(2)}) async-start(bf16[16,24,1280]{2,1,0:T(8,128)(2,1)} %maximum_maximum_fusion), calls=%async_computation.1 | async-start | bytes 1966080 | tf_op jit(solution)/shard_map/all_to_all | solution.py:508
  116.9 27.1 %copy-start.11 = (f32[128,640]{1,0:T(8,128)S(1)}, f32[128,640]{1,0:T(8,128)}, u32[]{:S(2)}) copy-start(f32[128,640]{1,0:T(8,128)} %get-tuple-element.32) | copy-start | bytes 983044
  116.9 27.1 %copy-start.12 = (f32[128,640]{1,0:T(8,128)S(1)}, f32[128,640]{1,0:T(8,128)}, u32[]{:S(2)}) copy-start(f32[128,640]{1,0:T(8,128)} %get-tuple-element.33) | copy-start | bytes 983044
  117.8 26.2 %collective-permute-start.8 = (bf16[128,1280]{1,0:T(8,128)(2,1)}, bf16[128,1280]{1,0:T(8,128)(2,1)S(1)}, u32[]{:S(2)}, u32[]{:S(2)}) collective-permute-start(bf16[128,1280]{1,0:T(8,128)(2,1)} %get-tuple-element.56), channel_id=1, source_target_pairs={{2,0},{3,1},{4,2},{5,3},{6,4},{7,5},{8,6},{9,7},{10,8},{11,9},{12,... | collective-permute-start | bytes 983048 | tf_op jit(solution)/shard_map/ppermute | solution.py:498
  119.1 24.9 %collective-permute-start.9 = (bf16[128,1280]{1,0:T(8,128)(2,1)S(1)}, bf16[128,1280]{1,0:T(8,128)(2,1)S(1)}, u32[]{:S(2)}, u32[]{:S(2)}) collective-permute-start(bf16[128,1280]{1,0:T(8,128)(2,1)S(1)} %get-tuple-element.57), channel_id=1, source_target_pairs={{4,0},{5,1},{6,2},{7,3},{8,4},{9,5},{10,6},{11,7},{12,8},{13,9},{1... | collective-permute-start | bytes 983048 | tf_op jit(solution)/shard_map/ppermute | solution.py:498
  132.8 11.2 %copy-start.8 = (bf16[16,24,1280]{2,1,0:T(8,128)(2,1)}, bf16[16,24,1280]{2,1,0:T(8,128)(2,1)S(1)}, u32[]{:S(2)}) copy-start(bf16[16,24,1280]{2,1,0:T(8,128)(2,1)S(1)} %all-to-all-done.1) | copy-start | bytes 2949124
  133.7 18.6 %all-to-all-start.2 = ((bf16[16,8,1280]{2,1,0:T(8,128)(2,1)}), bf16[16,8,1280]{2,1,0:T(8,128)(2,1)}, u32[]{:S(2)}, u32[]{:S(2)}) async-start(bf16[16,8,1280]{2,1,0:T(8,128)(2,1)} %broadcast_in_dim.34), calls=%async_computation.2 | async-start | bytes 655360 | tf_op jit(solution)/shard_map/all_to_all | solution.py:508
  145.0 21.8 %copy-start.1 = (bf16[6144,192]{0,1:T(8,128)(2,1)S(1)}, bf16[6144,192]{0,1:T(8,128)(2,1)}, u32[]{:S(2)}) copy-start(bf16[6144,192]{0,1:T(8,128)(2,1)} %param.14) | copy-start | bytes 7077892
  145.0 21.9 %copy-start.3 = (bf16[4096,128]{1,0:T(8,128)(2,1)S(1)}, bf16[4096,128]{1,0:T(8,128)(2,1)}, u32[]{:S(2)}) copy-start(bf16[4096,128]{1,0:T(8,128)(2,1)} %wv_ref.3) | copy-start | bytes 3145732
  152.4 13.4 %collective-permute-start.12 = (bf16[16,8,1280]{2,1,0:T(8,128)(2,1)}, bf16[16,8,1280]{2,1,0:T(8,128)(2,1)S(1)}, u32[]{:S(2)}, u32[]{:S(2)}) collective-permute-start(bf16[16,8,1280]{2,1,0:T(8,128)(2,1)} %all-to-all-done.2), channel_id=1, source_target_pairs={{0,1},{1,0},{2,3},{3,2},{4,5},{5,4},{6,7},{7,6},{8,9},{9,8},{10,11... | collective-permute-start | bytes 983048 | tf_op jit(solution)/shard_map/ppermute | solution.py:502
  168.6 7.0 %collective-permute-start.15 = (bf16[192,384]{1,0:T(8,128)(2,1)S(1)}, bf16[192,384]{1,0:T(8,128)(2,1)S(1)}, u32[]{:S(2)}, u32[]{:S(2)}) collective-permute-start(bf16[192,384]{1,0:T(8,128)(2,1)S(1)} %get-tuple-element.41), channel_id=1, source_target_pairs={{0,96},{32,0},{64,32},{96,64},{1,97},{33,1},{65,33},{97,65},{2,98}... | collective-permute-start | bytes 442376 | tf_op jit(solution)/shard_map/ppermute | solution.py:498
  172.5 9.5 %collective-permute-start.14 = (bf16[192,384]{1,0:T(8,128)(2,1)S(1)}, bf16[192,384]{1,0:T(8,128)(2,1)S(1)}, u32[]{:S(2)}, u32[]{:S(2)}) collective-permute-start(bf16[192,384]{1,0:T(8,128)(2,1)S(1)} %get-tuple-element.41), channel_id=1, source_target_pairs={{0,32},{32,64},{64,96},{96,0},{1,33},{33,65},{65,97},{97,1},{2,34}... | collective-permute-start | bytes 442376 | tf_op jit(solution)/shard_map/ppermute | solution.py:498
  172.5 9.5 %collective-permute-start.13 = (bf16[192,384]{1,0:T(8,128)(2,1)S(1)}, bf16[192,384]{1,0:T(8,128)(2,1)S(1)}, u32[]{:S(2)}, u32[]{:S(2)}) collective-permute-start(bf16[192,384]{1,0:T(8,128)(2,1)S(1)} %get-tuple-element.41), channel_id=1, source_target_pairs={{0,64},{32,96},{64,0},{96,32},{1,65},{33,97},{65,1},{97,33},{2,66}... | collective-permute-start | bytes 442376 | tf_op jit(solution)/shard_map/ppermute | solution.py:498
where the time goes:
time: 184 us; the launch traced here: 183 us
  Pallas kernels  64.1 us (35%)
  starting transfers between devices  52.5 us (29%)
  waiting for transfers between devices  35.6 us (19%)
  local copies, waits for them, and re-layouts  19.5 us (11%)
  other arithmetic  10.6 us (6%)
    pallas_call x2, Pallas kernels, attend_win(): pl.pallas_call(functools.partial(win_kernel, dh=dh, dv=dv, pair=pair), gr...  42.1 us
    all_to_all x3, waiting for transfers between devices, between_chips(): lax.all_to_all(array, 'seq', 0, 0, axis_index_groups=rings, tiled=True)  22.2 us
    ppermute x8, starting transfers between devices, shifted(): return lax.ppermute(array, axis, pairs)  19.6 us
    ppermute x8, starting transfers between devices, to_sibling(): lax.ppermute(array, 'seq', [(i, i ^ 1) for i in range(lax.axis_size('seq'...  19.2 us
    pallas_call x1, Pallas kernels, attend_cmp(): pl.pallas_call(functools.partial(cmp_kernel, dh=dh, dv=dv), grid=(groups,...  18.9 us
    all_to_all x3, starting transfers between devices, between_chips(): lax.all_to_all(array, 'seq', 0, 0, axis_index_groups=rings, tiled=True)  13.6 us
    ppermute x8, waiting for transfers between devices, shifted(): return lax.ppermute(array, axis, pairs)  13.3 us
    unnamed x44, local copies, waits for them, and re-layouts  5.93 us
  transfers between devices with their start and end apart: 19, of which 7 were waited for; matrix products, arithmetic and copies ran while one was open for 11% of the time, Pallas kernels for 33%

commit v1 on v0

v1 whole, which is shorter than its diff:
```python
import functools
import functools
import math
import jax
import jax.numpy as jnp
from jax import lax
from jax.experimental import pallas as pl
from jax.experimental.pallas import tpu as pltpu
from jax.sharding import PartitionSpec as P


BLK = 32
STRIDE = 16
WIN = 512
NEG = -1e30
QB = 32


def stack_rows(ref, row, width, starts):
    parts = [ref[row : row + QB, at : at + width] for at in starts]
    return jnp.concatenate(parts, axis=0)


def nt(a, b):
    return lax.dot_general(a, b, (((1,), (1,)), ((), ())), preferred_element_type=jnp.float32)


def nn(a, b):
    return lax.dot_general(a, b, (((1,), (0,)), ((), ())), preferred_element_type=jnp.float32)


def lay_keys(pair, ke, ko, kt, rows, odd_group, dh):
    def even():
        lane = lax.broadcasted_iota(jnp.int32, (pair.shape[0], 256), 1)
        src = pair[:, :256].astype(jnp.float32)
        low = jnp.where(lane < dh, src, 0.0)
        ke[rows, :] = low.astype(jnp.bfloat16)
        ko[rows, :] = pltpu.roll(low, 256 - dh, 1).astype(jnp.bfloat16)
        kt[:, rows] = low.T[:dh].astype(jnp.bfloat16)

    def odd():
        lane = lax.broadcasted_iota(jnp.int32, (pair.shape[0], 256), 1)
        src = pair[:, 128:].astype(jnp.float32)
        high = jnp.where(lane >= 256 - dh, src, 0.0)
        low = pltpu.roll(high, dh, 1)
        ko[rows, :] = high.astype(jnp.bfloat16)
        ke[rows, :] = low.astype(jnp.bfloat16)
        kt[:, rows] = low.T[:dh].astype(jnp.bfloat16)

    pl.when(jnp.logical_not(odd_group))(even)
    pl.when(odd_group)(odd)


def join_keys_grad(acc_e, acc_o, scale, dh, odd_group, put):
    def even():
        lane = lax.broadcasted_iota(jnp.int32, acc_e.shape, 1)
        total = (acc_e[...] + pltpu.roll(acc_o[...], dh, 1)) * scale
        put(0, jnp.where(lane < dh, total, 0.0), False)

    def odd():
        lane = lax.broadcasted_iota(jnp.int32, acc_e.shape, 1)
        total = (acc_o[...] + pltpu.roll(acc_e[...], 256 - dh, 1)) * scale
        put(128, jnp.where(lane >= 256 - dh, total, 0.0), True)

    pl.when(jnp.logical_not(odd_group))(even)
    pl.when(odd_group)(odd)


PIECES = 1


class Unit:
    def __init__(self, load, gate, kx, vv, kt, vt, chunks, mask, valid, bufs, acc_k, acc_v, scale, emit):
        self.load, self.gate, self.kx, self.vv, self.kt, self.vt = load, gate, kx, vv, kt, vt
        self.chunks, self.mask, self.valid = chunks, mask, valid
        self.s, self.g, self.p, self.u, self.q, self.c = bufs
        self.acc_k, self.acc_v, self.scale, self.emit = acc_k, acc_v, scale, emit
        self.tops = []
        n = len(chunks)
        cuts = [n * k // PIECES for k in range(PIECES + 1)]
        self.pieces = [chunks[i:j] for i, j in zip(cuts[:-1], cuts[1:])]

    def scores(self):
        def start():
            self.q[...], self.c[...] = self.load()

        def one(piece):
            lo, hi = piece[0][0], piece[-1][1]
            all_s = nt(self.kx[lo:hi, :], self.q[...])
            for at, end in piece:
                s = self.mask(all_s[at - lo : end - lo] * (self.scale * math.log2(math.e)), at, end)
                self.s[at:end, :] = s
                top = jnp.max(s, axis=0, keepdims=True)
                ok = self.valid(at)
                self.tops.append(top if ok is None else jnp.where(ok, top, NEG))

        def two(piece):
            lo, hi = piece[0][0], piece[-1][1]
            self.g[lo:hi, :] = nt(self.vv[lo:hi, :], self.c[...])

        return [start] + [functools.partial(f, piece) for f in (one, two) for piece in self.pieces]

    def weights(self):
        def one(at, end):
            if at == self.chunks[0][0]:
                self.top = functools.reduce(jnp.maximum, self.tops)
                self.norm = jnp.zeros_like(self.top)
                self.mean = jnp.zeros_like(self.top)
            ok = self.valid(at)
            base = self.top if ok is None else jnp.where(ok, self.top, -NEG)
            e = jnp.exp2(self.s[at:end, :] - base)
            self.s[at:end, :] = e
            self.norm = self.norm + jnp.sum(e, axis=0, keepdims=True)
            self.mean = self.mean + jnp.sum(e * self.g[at:end, :], axis=0, keepdims=True)

        return [functools.partial(one, at, end) for at, end in self.chunks]

    def grads(self):
        def one(at, end):
            if at == self.chunks[0][0]:
                self.mean = self.mean / self.norm
                self.weight = self.gate() / self.norm
                for lo, hi in ((0, self.chunks[0][0]), (self.chunks[-1][1], self.s.shape[0])):
                    if hi > lo:
                        self.p[lo:hi, :] = jnp.zeros((hi - lo, 256), jnp.bfloat16)
                        self.u[lo:hi, :] = jnp.zeros((hi - lo, 256), jnp.bfloat16)
            p = self.s[at:end, :] * self.weight
            self.p[at:end, :] = p.astype(jnp.bfloat16)
            self.u[at:end, :] = (p * (self.g[at:end, :] - self.mean)).astype(jnp.bfloat16)

        return [functools.partial(one, at, end) for at, end in self.chunks]

    def results(self):
        def values(piece):
            rows = slice(piece[0][0], piece[-1][1])
            self.acc_v[rows, :] += nn(self.p[rows, :], self.c[...])

        def keys(piece):
            rows = slice(piece[0][0], piece[-1][1])
            self.acc_k[rows, :] += nn(self.u[rows, :], self.q[...])

        def first():
            self.out = nn(self.vt[...], self.p[...])

        def second():
            self.emit(self.out, nn(self.kt[...], self.u[...]) * self.scale, self.mean)

        return [functools.partial(f, piece) for f in (values, keys) for piece in self.pieces] + [first, second]


def merge(one, two):
    steps = [((n + 0.5) / len(x), k, f) for k, x in enumerate((one, two)) for n, f in enumerate(x)]
    return [f for _, _, f in sorted(steps, key=lambda x: x[:2])]


def run_units(units):
    for f in units[0].scores():
        f()
    for n, unit in enumerate(units):
        before = units[n - 1].results() if n else []
        after = units[n + 1].scores() if n + 1 < len(units) else []
        for f in merge(unit.weights() + unit.grads(), before + after):
            f()
    for f in units[-1].results():
        f()


def cmp_kernel(place_ref, q_ref, c_ref, gate_ref, ck_ref, dk_ref, cv_ref, dv_ref, o_ref, dq_ref, gg_ref, gmine_ref, gother_ref,
               ke, ko, vv, kt, vt, s_e, s_o, g_e, g_o, p_e, p_o, u_e, u_o, q_e, q_o, c_e, c_o, acc_e, acc_o, acc_v, acc_w, *, dh, dv):
    group = pl.program_id(0)
    odd_group = group % 2 == 1
    scale = 1.0 / math.sqrt(dh)
    half = ck_ref.shape[0]
    rows = 2 * half
    tokens = q_ref.shape[0]
    for n, (k, v) in enumerate(((ck_ref, cv_ref), (dk_ref, dv_ref))):
        lay_keys(k, ke, ko, kt, slice(n * half, (n + 1) * half), odd_group, dh)
        vv[n * half : (n + 1) * half, :] = v[...]
    vt[...] = vv[...].astype(jnp.float32).T.astype(jnp.bfloat16)
    for acc in (acc_e, acc_o, acc_v, acc_w):
        acc[...] = jnp.zeros_like(acc)
    chunks = [(at, at + 128) for at in range(0, rows, 128)]
    heads = q_ref.shape[1] // dh // 2
    units = []

    def load(row, par):
        return (
            stack_rows(q_ref, row, 256, [2 * dh * h + par * 128 for h in range(heads)]),
            stack_rows(c_ref, row, dv, [(2 * h + par) * dv for h in range(heads)]),
        )

    for block in range(tokens // QB):
        row = block * QB
        lane = lax.broadcasted_iota(jnp.int32, (1, 256), 1) & (QB - 1)
        limit = (place_ref[0] * tokens + row + 1 + lane) // STRIDE

        def mask(s, at, end, limit=limit):
            index = lax.broadcasted_iota(jnp.int32, (end - at, 256), 0)
            owner = place_ref[1] if at < half else 1 - place_ref[1]
            index = 2 * (index - (index & 7)) + (index & 7) + 2 * (at % half) + 8 * owner
            return jnp.where(index <= limit, s, NEG)

        for par, (kx, bufs, acc, accv) in enumerate(
            ((ke, (s_e, g_e, p_e, u_e, q_e, c_e), acc_e, acc_v), (ko, (s_o, g_o, p_o, u_o, q_o, c_o), acc_o, acc_w))
        ):
            at = 2 * block + par

            def emit(out, dq, mean, at=at, block=block, par=par):
                gg_ref[0, at : at + 1, :] = mean
                o_ref[0, at] = out.astype(jnp.bfloat16)
                dq_ref[0, block, par * dh : (par + 1) * dh, :] = dq.astype(jnp.bfloat16)

            units.append(Unit(
                functools.partial(load, row, par),
                functools.partial(lambda at: gate_ref[0, at : at + 1, :], at),
                kx, vv, kt, vt, chunks, mask, lambda at: None, bufs, acc, accv, scale, emit,
            ))
    run_units(units)
    base = pl.multiple_of((group // 2) * 2 * dh, 128)

    def put(at, value, add):
        for ref, part in ((gmine_ref, value[:half]), (gother_ref, value[half:])):
            if add:
                ref[:, pl.ds(base + at, 128)] = (ref[:, pl.ds(base + at, 128)].astype(jnp.float32) + part[:, :128]).astype(jnp.bfloat16)
                ref[:, pl.ds(base + at + 128, 128)] = part[:, 128:].astype(jnp.bfloat16)
            else:
                ref[:, pl.ds(base + at, 256)] = part.astype(jnp.bfloat16)

    join_keys_grad(acc_e, acc_o, scale, dh, odd_group, put)
    at = pl.multiple_of(4 * dh + group * dv, 128)
    total = acc_v[...] + acc_w[...]
    gmine_ref[:, pl.ds(at, dv)] = total[:half].astype(jnp.bfloat16)
    gother_ref[:, pl.ds(at, dv)] = total[half:].astype(jnp.bfloat16)


def win_kernel(place_ref, q_ref, c_ref, gate_ref, k_ref, v_ref, four, four_mate, two, two_mate, mate, oc_ref, dqc_ref, *refs, dh, dv, pair):
    refs = refs[7:] if pair else refs
    halos = ((four, four), (four_mate, two_mate), (two, two), (two_mate, mate))
    win_body(place_ref, q_ref, c_ref, gate_ref, k_ref, v_ref, halos, oc_ref, dqc_ref, *refs, dh=dh, dv=dv, pair=pair)


def win_body(place_ref, q_ref, c_ref, gate_ref, k_ref, v_ref, halo_refs, oc_ref, dqc_ref,
             o_ref, dq_ref, gg_ref, g4_ref, g3_ref, g2_ref, g1_ref, gown_ref,
             ke, ko, vv, kt, vt, s_e, s_o, g_e, g_o, p_e, p_o, u_e, u_o, q_e, q_o, c_e, c_o, acc_e, acc_o, acc_v, acc_w, *, dh, dv, pair):
    odd_group = pl.program_id(0) == 1
    scale = 1.0 / math.sqrt(dh)
    tokens = q_ref.shape[0]
    lead = WIN
    base = pair * 2 * dh
    vbase = pl.multiple_of(4 * dh + (2 * pair + pl.program_id(0)) * dv, 128)
    first_core = place_ref[1] == 0
    for n, (a, b) in enumerate(halo_refs):
        rows = slice(n * tokens, (n + 1) * tokens)
        take = lambda at, width: a[:, pl.ds(at, width)] if a is b else jnp.where(first_core, a[:, pl.ds(at, width)], b[:, pl.ds(at, width)])
        lay_keys(take(base, 2 * dh), ke, ko, kt, rows, odd_group, dh)
        vv[rows, :] = take(vbase, dv)
    lay_keys(k_ref, ke, ko, kt, slice(lead, lead + tokens), odd_group, dh)
    vv[lead:, :] = v_ref[...]
    vt[...] = vv[...].astype(jnp.float32).T.astype(jnp.bfloat16)
    for acc in (acc_e, acc_o, acc_v, acc_w):
        acc[...] = jnp.zeros_like(acc)
    heads = q_ref.shape[1] // dh // 2

    def valid(at):
        return None if at >= lead else at >= lead - place_ref[0] * tokens

    units, halves = [], {}

    def load(row, par):
        return (
            stack_rows(q_ref, row, 256, [2 * dh * h + par * 128 for h in range(heads)]),
            stack_rows(c_ref, row, dv, [(2 * h + par) * dv for h in range(heads)]),
        )

    for block in range(tokens // QB):
        row = block * QB
        edges = sorted({row, row + QB, 128, 256, 384, 512, lead + row, lead + row + QB} - {0})
        edges = [row] + [x for x in edges if row < x <= lead + row + QB]
        chunks = list(zip(edges[:-1], edges[1:]))
        lane = lax.broadcasted_iota(jnp.int32, (QB, 256), 1) & (QB - 1)
        sub = lax.broadcasted_iota(jnp.int32, (QB, 256), 0)

        def mask(s, at, end, row=row, lane=lane, sub=sub):
            if at == row and end == row + QB:
                return jnp.where(sub > lane, s, NEG)
            if at == lead + row:
                return jnp.where(sub <= lane, s, NEG)
            return s

        for par, (kx, bufs, acc, accv) in enumerate(
            ((ke, (s_e, g_e, p_e, u_e, q_e, c_e), acc_e, acc_v), (ko, (s_o, g_o, p_o, u_o, q_o, c_o), acc_o, acc_w))
        ):
            at = 2 * block + par

            def emit(out, dq, mean, at=at, block=block, par=par, row=row):
                gg_ref[0, at : at + 1, :] = mean
                out = (out + oc_ref[0, at].astype(jnp.float32)).T
                for h in range(heads):
                    o_ref[row : row + QB, (2 * h + par) * dv : (2 * h + par + 1) * dv] = out[h * QB : (h + 1) * QB].astype(jnp.bfloat16)
                dq = dq + dqc_ref[0, block, par * dh : (par + 1) * dh, :].astype(jnp.float32)
                if par == 0:
                    halves[block] = dq
                    return
                dq = jnp.concatenate([halves.pop(block), dq], axis=0).T
                for h in range(heads):
                    dq_ref[row : row + QB, 2 * dh * h : 2 * dh * (h + 1)] = dq[h * QB : (h + 1) * QB].astype(jnp.bfloat16)

            units.append(Unit(
                functools.partial(load, row, par),
                functools.partial(lambda at: gate_ref[0, at : at + 1, :], at),
                kx, vv, kt, vt, chunks, mask, valid, bufs, acc, accv, scale, emit,
            ))
    run_units(units)

    def put(at, value, add):
        for n, ref in enumerate((g4_ref, g3_ref, g2_ref, g1_ref, gown_ref)):
            part, kind = value[n * tokens : (n + 1) * tokens], ref.dtype
            if add:
                ref[:, at : at + 128] = (ref[:, at : at + 128].astype(jnp.float32) + part[:, :128]).astype(kind)
                ref[:, at + 128 : at + 256] = part[:, 128:].astype(kind)
            else:
                ref[:, at : at + 256] = part.astype(kind)

    join_keys_grad(acc_e, acc_o, scale, dh, odd_group, put)
    total = acc_v[...] + acc_w[...]
    vat = pl.multiple_of(2 * dh + pl.program_id(0) * dv, 128)
    for n, ref in enumerate((g4_ref, g3_ref, g2_ref, g1_ref, gown_ref)):
        ref[:, pl.ds(vat, dv)] = total[n * tokens : (n + 1) * tokens].astype(ref.dtype)


def scratch(keys, dh, dv):
    f32, b16 = jnp.float32, jnp.bfloat16
    return [
        pltpu.VMEM((keys, 256), b16), pltpu.VMEM((keys, 256), b16),
        pltpu.VMEM((keys, dv), b16),
        pltpu.VMEM((dh, keys), b16), pltpu.VMEM((dv, keys), b16),
        *[pltpu.VMEM((keys, 256), f32)] * 4, *[pltpu.VMEM((keys, 256), b16)] * 4,
        *[pltpu.VMEM((256, 256), b16)] * 2, *[pltpu.VMEM((256, dv), b16)] * 2,
        pltpu.VMEM((keys, 256), f32), pltpu.VMEM((keys, 256), f32),
        pltpu.VMEM((keys, dv), f32), pltpu.VMEM((keys, dv), f32),
    ]


def attend_cmp(place, q, c, gate, mine, other, groups, dh, dv):
    tokens, half = q.shape[0], mine.shape[0]
    blocks = 2 * half
    skip = groups * dh // dv
    wide, high = q.shape[1] // groups, c.shape[1] // groups
    steps = tokens // QB
    f32, b16 = jnp.float32, jnp.bfloat16
    return pl.pallas_call(
        functools.partial(cmp_kernel, dh=dh, dv=dv),
        grid=(groups,),
        in_specs=[
            pl.BlockSpec(memory_space=pltpu.SMEM),
            pl.BlockSpec((tokens, wide), lambda g: (0, g)),
            pl.BlockSpec((tokens, high), lambda g: (0, g)),
            pl.BlockSpec((1, 2 * steps, 256), lambda g: (g, 0, 0)),
            *[pl.BlockSpec((half, 2 * dh), lambda g: (0, g // 2))] * 2,
            *[pl.BlockSpec((half, dv), lambda g: (0, skip + g))] * 2,
        ],
        out_specs=[
            pl.BlockSpec((1, 2 * steps, dv, 256), lambda g: (g, 0, 0, 0)),
            pl.BlockSpec((1, steps, 2 * dh, 256), lambda g: (g, 0, 0, 0)),
            pl.BlockSpec((1, 2 * steps, 256), lambda g: (g, 0, 0)),
            *[pl.BlockSpec((half, groups * (dh + dv)), lambda g: (0, 0))] * 2,
        ],
        out_shape=[
            jax.ShapeDtypeStruct((groups, 2 * steps, dv, 256), b16),
            jax.ShapeDtypeStruct((groups, steps, 2 * dh, 256), b16),
            jax.ShapeDtypeStruct((groups, 2 * steps, 256), f32),
            *[jax.ShapeDtypeStruct((half, groups * (dh + dv)), b16)] * 2,
        ],
        scratch_shapes=scratch(blocks, dh, dv),
        compiler_params=pltpu.CompilerParams(dimension_semantics=("arbitrary",), vmem_limit_bytes=56 * 2**20),
        cost_estimate=pl.CostEstimate(flops=blocks * tokens * 64 * 1920, transcendentals=blocks * tokens * 64, bytes_accessed=30_000_000),
        name="attend_cmp",
    )(place, q, c, gate, mine, other, mine, other)


def attend_win(place, q, c, gate, k, v, halos, oc, dqc, groups, dh, dv, pair, before):
    tokens = q.shape[0]
    wide, high = q.shape[1] // groups, c.shape[1] // groups
    steps = tokens // QB
    both = groups * (dh + dv)
    half = 2 * (dh + dv)
    f32, b16 = jnp.float32, jnp.bfloat16
    at = 2 * pair
    whole = lambda shape: pl.BlockSpec(shape, lambda g: (0,) * len(shape))
    return pl.pallas_call(
        functools.partial(win_kernel, dh=dh, dv=dv, pair=pair),
        grid=(2,),
        in_specs=[
            pl.BlockSpec(memory_space=pltpu.SMEM),
            pl.BlockSpec((tokens, wide), lambda g: (0, at + g)),
            pl.BlockSpec((tokens, high), lambda g: (0, at + g)),
            pl.BlockSpec((1, 2 * steps, 256), lambda g: (at + g, 0, 0)),
            pl.BlockSpec((tokens, 2 * dh), lambda g: (0, pair)),
            pl.BlockSpec((tokens, dv), lambda g: (0, at + g)),
            *[whole((tokens, both))] * 5,
            pl.BlockSpec((1, 2 * steps, dv, 256), lambda g: (at + g, 0, 0, 0)),
            pl.BlockSpec((1, steps, 2 * dh, 256), lambda g: (at + g, 0, 0, 0)),
            *[pl.BlockSpec(memory_space=pl.ANY)] * len(before),
        ],
        out_specs=[
            pl.BlockSpec((tokens, high), lambda g: (0, at + g)),
            pl.BlockSpec((tokens, wide), lambda g: (0, at + g)),
            pl.BlockSpec((1, 2 * steps, 256), lambda g: (g, 0, 0)),
            *[pl.BlockSpec((tokens, half), lambda g: (0, pair))] * 5,
        ],
        out_shape=[
            jax.ShapeDtypeStruct(c.shape, b16),
            jax.ShapeDtypeStruct(q.shape, b16),
            jax.ShapeDtypeStruct((2, 2 * steps, 256), f32),
            *[jax.ShapeDtypeStruct((tokens, both), b16)] * 4,
            jax.ShapeDtypeStruct((tokens, both), f32),
        ],
        scratch_shapes=scratch(WIN + tokens, dh, dv),
        input_output_aliases={13: 0, 14: 1, 15: 3, 16: 4, 17: 5, 18: 6, 19: 7} if before else {},
        compiler_params=pltpu.CompilerParams(dimension_semantics=("arbitrary",), vmem_limit_bytes=56 * 2**20),
        cost_estimate=pl.CostEstimate(flops=320 * tokens * 64 * 1920, transcendentals=320 * tokens * 64, bytes_accessed=30_000_000),
        name="attend_win",
    )(place, q, c, gate, k, v, *halos, oc, dqc, *before)


def split_lanes(pair, dh, odd):
    lane = lax.broadcasted_iota(jnp.int32, (pair.shape[0], 256), 1)
    if odd:
        return jnp.where(lane >= 256 - dh, pair[:, 128:], 0.0)
    return jnp.where(lane < dh, pair[:, :256], 0.0)


def to_left(x, dh):
    return pltpu.roll(x, dh, 1)


def to_right(x, dh):
    return pltpu.roll(x, 256 - dh, 1)


def joined(left, right):
    return jnp.concatenate([left[:, :128], left[:, 128:] + right[:, :128], right[:, 128:]], axis=1)


def compress_kernel(k_ref, v_ref, prior_ref, wk_ref, wv_ref, out_ref, ext, y_scr, *, dh, dv, groups):
    tokens, kw = k_ref.shape
    tiles = ext.shape[0]
    for n in range(tiles):
        at = n * 128
        ext[n, :BLK, :] = prior_ref[:, at : at + 128].astype(jnp.float32)
        ref, at = (k_ref, at) if at < kw else (v_ref, at - kw)
        ext[n, BLK:, :] = ref[:, at : at + 128].astype(jnp.float32)

    def every(p):
        return jnp.concatenate([ext[n, pl.ds(p, blocks, stride=STRIDE), :] for n in range(tiles)], axis=1)

    blocks = tokens // STRIDE
    acc_k = jnp.zeros((groups * blocks, dh), jnp.float32)
    acc_v = jnp.zeros((groups * blocks, dv), jnp.float32)
    for p in range(0, BLK, 2):
        one, two = every(p), every(p + 1)
        rows = []
        for g in range(groups):
            at = (g // 2) * 2 * dh
            if g % 2 == 0:
                left = split_lanes(one[:, at : at + 2 * dh], dh, False)
                right = to_right(split_lanes(two[:, at : at + 2 * dh], dh, False), dh)
            else:
                left = to_left(split_lanes(one[:, at : at + 2 * dh], dh, True), dh)
                right = split_lanes(two[:, at : at + 2 * dh], dh, True)
            rows.append(joined(left, right))
        acc_k += nt(jnp.concatenate(rows, axis=0).astype(jnp.bfloat16), wk_ref[:, p * dh : (p + 2) * dh])
        vals = [
            jnp.concatenate([x[:, kw + g * dv : kw + (g + 1) * dv] for x in (one, two)], axis=1) for g in range(groups)
        ]
        acc_v += nn(jnp.concatenate(vals, axis=0).astype(jnp.bfloat16), wv_ref[p * dv : (p + 2) * dv, :])
    y_scr[...] = jnp.zeros_like(y_scr)
    y_scr[:, :dh] = acc_k
    for m in range(groups // 2):
        left = y_scr[2 * m * blocks : (2 * m + 1) * blocks, :]
        right = to_right(y_scr[(2 * m + 1) * blocks : (2 * m + 2) * blocks, :], dh)
        out_ref[:, 2 * m * dh : 2 * (m + 1) * dh] = joined(left, right).astype(jnp.bfloat16)
    for g in range(groups):
        out_ref[:, kw + g * dv : kw + (g + 1) * dv] = acc_v[g * blocks : (g + 1) * blocks].astype(jnp.bfloat16)


def compress(keys, values, prior, wk_t, wv, groups):
    dh, dv = wk_t.shape[0], wv.shape[1]
    blocks = keys.shape[0] // STRIDE
    both = keys.shape[1] + values.shape[1]
    return pl.pallas_call(
        functools.partial(compress_kernel, dh=dh, dv=dv, groups=groups),
        out_shape=jax.ShapeDtypeStruct((blocks, both), jnp.bfloat16),
        scratch_shapes=[
            pltpu.VMEM((both // 128, BLK + keys.shape[0], 128), jnp.float32),
            pltpu.VMEM((groups * blocks, 256), jnp.float32),
        ],
        compiler_params=pltpu.CompilerParams(vmem_limit_bytes=40 * 2**20),
        name="compress",
    )(keys, values, prior, wk_t, wv)


def back_kernel(place_ref, mine_ref, other_ref, got_ref, wk_ref, wv_ref, part_ref, back_ref, wide, spread, *, dh, dv, groups):
    half, both = mine_ref.shape
    blocks = 2 * half
    kw = groups * dh
    chunks = back_ref.shape[0] // STRIDE
    for ref, owner in ((mine_ref, place_ref[1]), (other_ref, 1 - place_ref[1])):
        value = ref[...].astype(jnp.float32)
        for n in range(0, half, chunks):
            wide[pl.ds(pl.multiple_of(2 * n + chunks * owner, chunks), chunks), :] = value[n : n + chunks]
    wide[blocks:, :] = jnp.zeros((wide.shape[0] - blocks, both), jnp.float32)
    shard = place_ref[0]
    lined = jnp.where(shard < STRIDE, wide[2 : blocks + 2, :], wide[1 : blocks + 1, :]).astype(jnp.bfloat16)
    flipped = got_ref[...].astype(jnp.float32)[:, chunks:].reshape(blocks, both).T.astype(jnp.bfloat16)
    square = jnp.zeros((2 * dh, 2 * dh), jnp.float32)
    for m in range(groups // 2):
        at = 2 * m * dh
        square += nn(flipped[at : at + 2 * dh], lined[:, at : at + 2 * dh])
    low = square[:dh, :256] + to_left(split_lanes(square[dh:], dh, True), dh)
    part_v = jnp.zeros((dv, dv), jnp.float32)
    for g in range(groups):
        at = kw + g * dv
        part_v += nn(flipped[at : at + dv], lined[:, at : at + dv])
    part_ref[:, :256] = low.astype(jnp.bfloat16)
    part_ref[:dv, 256:] = part_v.astype(jnp.bfloat16)
    part_ref[dv:, 256:] = jnp.zeros((dh - dv, dv), jnp.bfloat16)
    here = wide[pl.ds(pl.multiple_of(shard * chunks, 8), chunks + 8), :]
    near, far = here[1 : chunks + 1], here[2 : chunks + 2]

    def stacked(x):
        rows = []
        for g in range(groups):
            half = split_lanes(x[:, (g // 2) * 2 * dh : (g // 2 + 1) * 2 * dh], dh, g % 2 == 1)
            rows.append(half if g % 2 == 0 else to_left(half, dh))
        return jnp.concatenate(rows, axis=0)[:, :dh].astype(jnp.bfloat16)

    far_k, near_k = stacked(far), stacked(near)
    vals = lambda x: jnp.concatenate([x[:, kw + g * dv : kw + (g + 1) * dv] for g in range(groups)], axis=0).astype(jnp.bfloat16)
    far_v, near_v = vals(far), vals(near)
    span = STRIDE * dh
    for p in range(0, STRIDE, 2):
        at = p * dh
        got = nn(far_k, wk_ref[:, at : at + 2 * dh]) + nn(near_k, wk_ref[:, span + at : span + at + 2 * dh])
        for m in range(groups // 2):
            a = got[2 * m * chunks : (2 * m + 1) * chunks]
            b = got[(2 * m + 1) * chunks : (2 * m + 2) * chunks]
            one = joined(split_lanes(a, dh, False), to_right(split_lanes(b, dh, False), dh))
            two = joined(to_left(split_lanes(a, dh, True), dh), split_lanes(b, dh, True))
            for n in range(3):
                lanes = slice(n * 128, n * 128 + 128)
                spread[3 * m + n, pl.ds(p, chunks, stride=STRIDE), :] = one[:, lanes]
                spread[3 * m + n, pl.ds(p + 1, chunks, stride=STRIDE), :] = two[:, lanes]
    for p in range(STRIDE):
        at = p * dv
        got = nt(far_v, wv_ref[at : at + dv, :]) + nt(near_v, wv_ref[STRIDE * dv + at : STRIDE * dv + at + dv, :])
        for g in range(groups):
            spread[kw // 128 + g, pl.ds(p, chunks, stride=STRIDE), :] = got[g * chunks : (g + 1) * chunks]
    for n in range(spread.shape[0]):
        back_ref[:, n * 128 : n * 128 + 128] = spread[n]


def compress_back(place, mine, other, got, wk_t, wv, tokens, groups):
    dh, dv = wk_t.shape[0], wv.shape[1]
    half, both = mine.shape
    vmem = pl.BlockSpec(memory_space=pltpu.VMEM)
    return pl.pallas_call(
        functools.partial(back_kernel, dh=dh, dv=dv, groups=groups),
        in_specs=[pl.BlockSpec(memory_space=pltpu.SMEM), vmem, vmem, vmem, vmem, vmem],
        out_shape=[
            jax.ShapeDtypeStruct((dh, 256 + dv), jnp.bfloat16),
            jax.ShapeDtypeStruct((tokens, both), jnp.float32),
        ],
        scratch_shapes=[
            pltpu.VMEM((2 * half + 16, both), jnp.float32),
            pltpu.VMEM((both // 128, tokens, 128), jnp.float32),
        ],
        compiler_params=pltpu.CompilerParams(vmem_limit_bytes=40 * 2**20),
        name="compress_back",
    )(place, mine, other, got, wk_t, wv)


def gate_rows(gate, groups):
    tokens, heads = gate.shape
    cut = gate.reshape(tokens // QB, QB, groups, heads // groups // 2, 2)
    return cut.transpose(2, 0, 4, 3, 1).reshape(groups, 2 * (tokens // QB), -1)


def gate_columns(rows, tokens):
    groups = rows.shape[0]
    cut = rows.reshape(groups, tokens // QB, 2, -1, QB)
    return cut.transpose(1, 4, 0, 3, 2).reshape(tokens, -1)


def shifted(array, axis, by, wrap=False):
    devices = lax.axis_size(axis)
    if wrap:
        pairs = [(i, (i + by) % devices) for i in range(devices)]
    else:
        pairs = [(i, i + by) for i in range(devices) if 0 <= i + by < devices]
    return lax.ppermute(array, axis, pairs)


def to_sibling(array):
    return lax.ppermute(array, "seq", [(i, i ^ 1) for i in range(lax.axis_size("seq"))])


def between_chips(array):
    devices = lax.axis_size("seq")
    rings = [list(range(k, devices, 2)) for k in range(2)]
    return lax.all_to_all(array, "seq", 0, 0, axis_index_groups=rings, tiled=True)


def gathered(array):
    chips = lax.axis_size("seq") // 2
    mine = between_chips(jnp.broadcast_to(array[None], (chips, *array.shape))).reshape(-1, array.shape[1])
    return mine, to_sibling(mine)


def whole_step(queries, keys_in, values_in, gate_cmp, gate_win, cotangent, compress_key, compress_value):
    dh, dv = compress_key.shape[1], compress_value.shape[1]
    q, c, keys, values = queries[0], cotangent[0], keys_in[0], values_in[0]
    tokens, kw = keys.shape
    groups = kw // dh
    shards = lax.axis_size("seq")
    shard = lax.axis_index("seq").astype(jnp.int32)
    core = shard % 2
    place = jnp.stack([shard, core])
    wk_t = compress_key.T
    last = jnp.concatenate([keys[tokens - BLK :], values[tokens - BLK :]], axis=1)
    prior = shifted(last, "seq", 1)
    cmp_own = compress(keys, values, prior, wk_t, compress_value, groups)
    mine, other = gathered(cmp_own)
    late_keys, late_values, _ = lax.optimization_barrier((keys, values, cmp_own))
    own = jnp.concatenate([late_keys, late_values], axis=1)
    both = own.shape[1]
    two = shifted(own, "seq", 2)
    four = shifted(own, "seq", 4)
    mate = to_sibling(own)
    two_mate = to_sibling(two)
    four_mate = to_sibling(four)
    halos = [four, four_mate, two, two_mate, mate]
    oc, dqc, ggc, gmine, gother = attend_cmp(place, q, c, gate_rows(gate_cmp[0], groups), mine, other, groups, dh, dv)
    chip = jnp.where(core == 0, jnp.stack([own, mate]), jnp.stack([mate, own]))
    chip = chip.reshape(2 * tokens // STRIDE, STRIDE // 2, 2, both)
    residue = jnp.where(core == 0, chip[:, :, 0], chip[:, :, 1]).transpose(1, 0, 2)
    residue = jnp.concatenate([residue, residue], axis=0)
    folded = to_sibling(gother)
    blocks_dev = cmp_own.shape[0]
    folded = (folded.astype(jnp.float32) + gmine.astype(jnp.float32)).astype(jnp.bfloat16)
    sent = jnp.concatenate([folded.reshape(shards // 2, blocks_dev, both), residue], axis=1)
    got = between_chips(sent)
    gckb = jnp.sum(got[:, :blocks_dev].astype(jnp.float32), axis=0).astype(jnp.bfloat16)
    grads = gathered(gckb)
    win = functools.partial(attend_win, place, q, c, gate_rows(gate_win[0], groups), keys, values, halos, oc, dqc, groups, dh, dv)
    ggw, before = [], ()
    for pair in range(groups // 2):
        attended, grad_query, gg, *gk = win(pair, before)
        ggw.append(gg)
        before = (attended, grad_query, *gk)
    to_behind4, to_behind3, to_behind2, to_behind1, keep = gk
    near, nearest = to_sibling(to_behind3), to_sibling(to_behind1)
    near, nearest = near.astype(jnp.float32), nearest.astype(jnp.float32)
    to_four = (to_behind4.astype(jnp.float32) + jnp.where(core == 0, 0.0, near)).astype(jnp.bfloat16)
    to_two = (to_behind2.astype(jnp.float32) + jnp.where(core == 0, near, nearest)).astype(jnp.bfloat16)
    from_four, from_two = shifted(to_four, "seq", -4), shifted(to_two, "seq", -2)
    keep = keep + jnp.where(core == 0, nearest, 0.0)
    keep = keep + from_two.astype(jnp.float32) + from_four.astype(jnp.float32)
    half = 2 * (dh + dv)
    keys_back = jnp.concatenate([keep[:, at : at + 2 * dh] for at in (0, half)], axis=1)
    values_back = jnp.concatenate([keep[:, at + 2 * dh : at + half] for at in (0, half)], axis=1)
    part, back = compress_back(place, *grads, got, wk_t, compress_value, tokens, groups)
    parts = [shifted(part, "dp", by, True).astype(jnp.float32) for by in (1, 2, 3)]
    total = (part.astype(jnp.float32) + parts[1]) + (parts[0] + parts[2])
    grad_key = keys_back + back[:, :kw]
    grad_value = values_back + back[:, kw:]
    return (
        attended[None],
        grad_query[None],
        grad_key.astype(jnp.bfloat16)[None],
        grad_value.astype(jnp.bfloat16)[None],
        gate_columns(ggc, tokens)[None],
        gate_columns(jnp.concatenate(ggw, axis=0), tokens)[None],
        total[:, :dh],
        total[:dv, 256:],
    )


def solution(mesh):
    split, copied, rows = P("dp", "seq", None), P(), P("seq", None)
    return jax.shard_map(
        whole_step,
        mesh=mesh,
        in_specs=(split,) * 6 + (copied,) * 2,
        out_specs=(split,) * 6 + (rows,) * 2,
        check_vma=False,
    )
```

time: 184 us -> 169 us (0.918)
  Pallas kernels: 64.1 us -> 49.6 us
  starting transfers between devices: 52.5 us -> 56.3 us
  other arithmetic: 10.6 us -> 7.14 us
    pallas_call x2, Pallas kernels: 42.1 us -> 31.2 us  [attend_win(): pl.pallas_call(functools.partial(win_kernel, dh=dh, dv=dv, pair=pair), gr...]
    all_to_all x3, waiting for transfers between devices: 22.2 us -> 15 us  [between_chips(): lax.all_to_all(array, 'seq', 0, 0, axis_index_groups=rings, tiled=True)]
    ppermute x8, waiting for transfers between devices: 13.3 us -> 20.5 us  [shifted(): return lax.ppermute(array, axis, pairs)]
    all_to_all x3, starting transfers between devices: 13.6 us -> 20.7 us  [between_chips(): lax.all_to_all(array, 'seq', 0, 0, axis_index_groups=rings, tiled=True)]
    pallas_call x1, Pallas kernels: 18.9 us -> 14.3 us  [attend_cmp(): pl.pallas_call(functools.partial(cmp_kernel, dh=dh, dv=dv), grid=(groups,...]
    select_n x3 -> x0, other arithmetic: 4.27 us -> none  [the longest x2 3.16 us: gathered(): jnp.where(core == 0, jnp.stack([mine, other], axis=1), jnp.stack([other,...]
    ppermute x8, starting transfers between devices: 19.2 us -> 15.8 us  [to_sibling(): lax.ppermute(array, 'seq', [(i, i ^ 1) for i in range(lax.axis_size('seq'...]
    slice x2 -> x0, local copies, waits for them, and re-layouts: 2.48 us -> none  [the longest x1 1.34 us: whole_step(): gh[n * tokens:(n + 1) * tokens]]
  transfers between devices with their start and end apart: 19 -> 19, of which waited for: 7 -> 8; matrix products, arithmetic and copies ran while one was open for 11% -> 9% of each run, Pallas kernels for 33% -> 27%
where the time goes in v1:
time: 169 us; the launch traced here: 168 us
  starting transfers between devices  56.3 us (33%)
  Pallas kernels  49.6 us (29%)
  waiting for transfers between devices  35.5 us (21%)
  local copies, waits for them, and re-layouts  18.6 us (11%)
  other arithmetic  7.14 us (4%)
    pallas_call x2, Pallas kernels, attend_win(): pl.pallas_call(functools.partial(win_kernel, dh=dh, dv=dv, pair=pair), gr...  31.2 us
    all_to_all x3, starting transfers between devices, between_chips(): lax.all_to_all(array, 'seq', 0, 0, axis_index_groups=rings, tiled=True)  20.7 us
    ppermute x8, waiting for transfers between devices, shifted(): return lax.ppermute(array, axis, pairs)  20.5 us
    ppermute x8, starting transfers between devices, shifted(): return lax.ppermute(array, axis, pairs)  19.8 us
    ppermute x8, starting transfers between devices, to_sibling(): lax.ppermute(array, 'seq', [(i, i ^ 1) for i in range(lax.axis_size('seq'...  15.8 us
    all_to_all x3, waiting for transfers between devices, between_chips(): lax.all_to_all(array, 'seq', 0, 0, axis_index_groups=rings, tiled=True)  15 us
    pallas_call x1, Pallas kernels, attend_cmp(): pl.pallas_call(functools.partial(cmp_kernel, dh=dh, dv=dv), grid=(groups,...  14.3 us
    unnamed x47, local copies, waits for them, and re-layouts  7.6 us
  transfers between devices with their start and end apart: 19, of which 8 were waited for; matrix products, arithmetic and copies ran while one was open for 9% of the time, Pallas kernels for 27%

profile of v1, /device:TPU:1, one launch (start us, length us, event | category | flops | bytes accessed | tf_op | source)
XLA Modules:
  0.0 168.3 jit_solution(2294902830273115808)
XLA Ops:
  0.6 0.8 slice_bitcast_fusion.1
  1.4 0.8 slice_bitcast_fusion
  2.2 4.6 %collective-permute-start = (bf16[32,1280]{1,0:T(8,128)(2,1)S(1)}, bf16[32,1280]{1,0:T(8,128)(2,1)S(1)}, u32[]{:S(2)}, u32[]{:S(2)}) collective-permute-start(bf16[32,1280]{1,0:T(8,128)(2,1)S(1)} %pad_maximum_fusion), channel_id=1, source_target_pairs={{0,1},{1,2},{2,3},{3,4},{4,5},{5,6},{6,7},{7,8},{8,9},{9,10},{10,1... | collective-permute-start | bytes 245768 | tf_op jit(solution)/shard_map/ppermute | solution.py:601
  6.8 1.5 collective-permute-done.prior_ref
  8.3 1.7 copy-done
  9.9 1.2 copy-done.2
  11.2 0.9 copy-done.4
  12.1 0.9 copy-done.5
  13.0 1.4 compress.1
  14.4 0.1 collective-permute-start.5
  14.5 0.7 broadcast_in_dim.30
  15.3 7.9 %all-to-all-start = ((bf16[16,8,1280]{2,1,0:T(8,128)(2,1)}), bf16[16,8,1280]{2,1,0:T(8,128)(2,1)S(1)}, u32[]{:S(2)}, u32[]{:S(2)}) async-start(bf16[16,8,1280]{2,1,0:T(8,128)(2,1)} %broadcast_in_dim.30), calls=%async_computation | async-start | bytes 655360 | tf_op jit(solution)/shard_map/all_to_all | solution.py:611
  23.2 0.1 reshape_squeeze.7
  23.4 0.7 reshape.49.gate_ref
  24.1 0.1 reshape_squeeze.6
  24.3 0.7 reshape.48.gate_ref
  25.0 3.3 %collective-permute-start.3 = (bf16[128,1280]{1,0:T(8,128)(2,1)S(1)}, bf16[128,1280]{1,0:T(8,128)(2,1)S(1)}, u32[]{:S(2)}, u32[]{:S(2)}) collective-permute-start(bf16[128,1280]{1,0:T(8,128)(2,1)S(1)} %constant_dynamic-update-slice_fusion), channel_id=1, source_target_pairs={{0,2},{1,3},{2,4},{3,5},{4,6},{5,7},{6,8},{7,9},{8,10},{9,11},{10,... | collective-permute-start | bytes 983048 | tf_op jit(solution)/shard_map/ppermute | solution.py:601
  28.2 0.6 pad_add_fusion.place_ref
  28.8 4.3 %collective-permute-start.1 = (bf16[128,1280]{1,0:T(8,128)(2,1)S(1)}, bf16[128,1280]{1,0:T(8,128)(2,1)S(1)}, u32[]{:S(2)}, u32[]{:S(2)}) collective-permute-start(bf16[128,1280]{1,0:T(8,128)(2,1)S(1)} %constant_dynamic-update-slice_fusion), channel_id=1, source_target_pairs={{0,4},{1,5},{2,6},{3,7},{4,8},{5,9},{6,10},{7,11},{8,12},{9,13},{1... | collective-permute-start | bytes 983048 | tf_op jit(solution)/shard_map/ppermute | solution.py:601
  33.1 1.2 collective-permute-start.6
  34.4 0.1 maximum_select_fusion
  34.5 0.2 select_n.58
  34.7 0.7 collective-permute-done.3.two
  35.4 1.9 %collective-permute-start.4 = (bf16[128,1280]{1,0:T(8,128)(2,1)S(1)}, bf16[128,1280]{1,0:T(8,128)(2,1)S(1)}, u32[]{:S(2)}, u32[]{:S(2)}) collective-permute-start(bf16[128,1280]{1,0:T(8,128)(2,1)S(1)} %collective-permute-done.3.two), channel_id=1, source_target_pairs={{0,1},{1,0},{2,3},{3,2},{4,5},{5,4},{6,7},{7,6},{8,9},{9,8},{10,11... | collective-permute-start | bytes 983048 | tf_op jit(solution)/shard_map/ppermute | solution.py:605
  37.3 0.9 fusion.15
  38.2 4.2 %collective-permute-done.1.four = bf16[128,1280]{1,0:T(8,128)(2,1)S(1)} collective-permute-done((bf16[128,1280]{1,0:T(8,128)(2,1)S(1)}, bf16[128,1280]{1,0:T(8,128)(2,1)S(1)}, u32[]{:S(2)}, u32[]{:S(2)}) %collective-permute-start.1) | collective-permute-done | bytes 327712 | tf_op jit(solution)/shard_map/ppermute | solution.py:601
  42.5 1.2 collective-permute-start.2
  43.6 0.4 fusion.9
  44.0 0.7 copy-done.22
  44.7 14.3 %attend_cmp.1 = (bf16[4,8,128,256]{3,2,1,0:T(8,128)(2,1)}, bf16[4,4,384,256]{3,2,1,0:T(8,128)(2,1)}, f32[4,8,256]{2,1,0:T(8,128)}, bf16[128,1280]{1,0:T(8,128)(2,1)}, bf16[128,1280]{1,0:T(8,128)(2,1)}) custom-call(s32[2]{0:T(128)} %pad_add_fusion.place_ref, bf16[128,12288]{1,0:T(8,128)(2,1)} %bitcast.57, bf16[128,8192]{1,0:T(8,128)(2,1)} %bitcast.61, ...), custom_call_target="tpu_custom_call" | custom-call | flops 4026531840 | bytes 30000000 | tf_op jit(solution)/shard_map/attend_cmp/pallas_call | solution.py:351
  59.0 0.1 collective-permute-start.11
  59.2 0.7 copy-done.15
  59.9 0.1 copy-done.16
  60.0 15.7 %attend_win.2 = (bf16[128,8192]{1,0:T(8,128)(2,1)}, bf16[128,12288]{1,0:T(8,128)(2,1)}, f32[2,8,256]{2,1,0:T(8,128)}, bf16[128,1280]{1,0:T(8,128)(2,1)}, bf16[12...) custom-call(s32[2]{0:T(128)} %pad_add_fusion.place_ref, ...), custom_call_target="tpu_custom_call" | custom-call | flops 5033164800 | bytes 30000000 | tf_op jit(solution)/shard_map/attend_win/pallas_call | solution.py:390
  75.7 15.6 %attend_win.3 = (bf16[128,8192]{1,0:T(8,128)(2,1)}, bf16[128,12288]{1,0:T(8,128)(2,1)}, f32[2,8,256]{2,1,0:T(8,128)}, bf16[128,1280]{1,0:T(8,128)(2,1)}, bf16[12...) custom-call(s32[2]{0:T(128)} %pad_add_fusion.place_ref, ...), custom_call_target="tpu_custom_call", output_to_operand_aliasing={{0}: (13, {}), {1}: (14, {}), {3}: (15, {}), {4}: (16, {}),... | custom-call | flops 5033164800 | bytes 30000000 | tf_op jit(solution)/shard_map/attend_win/pallas_call | solution.py:390
  91.3 0.8 collective-permute-start.7
  92.1 0.1 collective-permute-start.8
  92.3 1.1 maximum_maximum_fusion
  93.3 8.4 %all-to-all-start.1 = ((bf16[16,24,1280]{2,1,0:T(8,128)(2,1)}), bf16[16,24,1280]{2,1,0:T(8,128)(2,1)S(1)}, u32[]{:S(2)}, u32[]{:S(2)}) async-start(bf16[16,24,1280]{2,1,0:T(8,128)(2,1)} %maximum_maximum_fusion), calls=%async_computation.1 | async-start | bytes 1966080 | tf_op jit(solution)/shard_map/all_to_all | solution.py:611
  101.8 1.0 fusion.4
  102.8 1.3 collective-permute-start.9
  104.1 1.3 collective-permute-start.10
  105.4 0.1 reshape.53
  105.5 0.7 broadcast_in_dim_reshape.6
  106.4 0.7 broadcast_in_dim_reshape.7
  107.2 9.9 %all-to-all-done.1.got_ref = bf16[16,24,1280]{2,1,0:T(8,128)(2,1)S(1)} async-done(((bf16[16,24,1280]{2,1,0:T(8,128)(2,1)}), bf16[16,24,1280]{2,1,0:T(8,128)(2,1)S(1)}, u32[]{:S(2)}, u32[]{:S(2)}) %all-to-all-start.1) | async-done | bytes 983072 | tf_op jit(solution)/shard_map/all_to_all | solution.py:611
  117.1 0.8 broadcast_in_dim.34
  117.9 4.3 %all-to-all-start.2 = ((bf16[16,8,1280]{2,1,0:T(8,128)(2,1)}), bf16[16,8,1280]{2,1,0:T(8,128)(2,1)}, u32[]{:S(2)}, u32[]{:S(2)}) async-start(bf16[16,8,1280]{2,1,0:T(8,128)(2,1)} %broadcast_in_dim.34), calls=%async_computation.2 | async-start | bytes 655360 | tf_op jit(solution)/shard_map/all_to_all | solution.py:611
  122.2 7.3 %collective-permute-done.9 = bf16[128,1280]{1,0:T(8,128)(2,1)} collective-permute-done((bf16[128,1280]{1,0:T(8,128)(2,1)}, bf16[128,1280]{1,0:T(8,128)(2,1)}, u32[]{:S(2)}, u32[]{:S(2)}) %collective-permute-start.9) | collective-permute-done | bytes 327712 | tf_op jit(solution)/shard_map/ppermute | solution.py:601
  129.6 2.4 %fusion.2 = f32[128,1280]{1,0:T(8,128)} fusion(f32[128,1280]{1,0:T(8,128)} %get-tuple-element.46, bf16[128,1280]{1,0:T(8,128)(2,1)} %copy-done.7, bf16[128,1280]{1,0:T(8,128)(2,1)} %collective-permute-done.10, bf16[128,1280]{1,0:T(8,128)(2,1)} %collective-permute-done.9, pred[]{:T(512)S(6)} %eq.4), kind=kLoop, calls=%fused_computation.6 | loop fusion | flops 1146880 | bytes 2293761 | tf_op jit(solution)/shard_map/add | solution.py:668
  131.9 5.1 %all-to-all-done.2 = bf16[16,8,1280]{2,1,0:T(8,128)(2,1)} async-done(((bf16[16,8,1280]{2,1,0:T(8,128)(2,1)}), bf16[16,8,1280]{2,1,0:T(8,128)(2,1)}, u32[]{:S(2)}, u32[]{:S(2)}) %all-to-all-start.2) | async-done | bytes 327712 | tf_op jit(solution)/shard_map/all_to_all | solution.py:611
  137.0 10.5 %collective-permute-start.12 = (bf16[128,1280]{1,0:T(8,128)(2,1)}, bf16[128,1280]{1,0:T(8,128)(2,1)S(1)}, u32[]{:S(2)}, u32[]{:S(2)}) collective-permute-start(bf16[128,1280]{1,0:T(8,128)(2,1)} %bitcast.19.mine_ref), channel_id=1, source_target_pairs={{0,1},{1,0},{2,3},{3,2},{4,5},{5,4},{6,7},{7,6},{8,9},{9,8},{10,11... | collective-permute-start | bytes 983048 | tf_op jit(solution)/shard_map/ppermute | solution.py:605
  147.5 1.0 fusion.13
  148.5 1.1 fusion.14
  149.6 1.2 copy-done.3
  150.8 2.7 %compress_back.1 = (bf16[192,384]{1,0:T(8,128)(2,1)S(1)}, f32[128,1280]{1,0:T(8,128)S(1)}) custom-call(s32[2]{0:T(128)S(1)} %copy-done.6, bf16[128,1280]{1,0:T(8,128)(2,1)} %bitcast.19.mine_ref, bf16[128,1280]{1,0:T(8,128)(2,1)S(1)} %collective-permute-done.12.other_ref, bf16[16,24,1280]{2,1,0:T(8,128)(2,1)S(1)} %all-to-all-done.1.got_ref, ...), custom_call_target="tpu_custom_call" | custom-call | tf_op jit(solution)/shard_map/compress_back/pallas_call | solution.py:567
  153.6 3.8 %collective-permute-start.15 = (bf16[192,384]{1,0:T(8,128)(2,1)S(1)}, bf16[192,384]{1,0:T(8,128)(2,1)S(1)}, u32[]{:S(2)}, u32[]{:S(2)}) collective-permute-start(bf16[192,384]{1,0:T(8,128)(2,1)S(1)} %get-tuple-element.57), channel_id=1, source_target_pairs={{0,96},{32,0},{64,32},{96,64},{1,97},{33,1},{65,33},{97,65},{2,98}... | collective-permute-start | bytes 442376 | tf_op jit(solution)/shard_map/ppermute | solution.py:601
  157.4 1.3 collective-permute-start.13
  158.7 0.7 fusion.11
  159.4 0.7 fusion.12
  160.1 0.5 collective-permute-done.15
  160.6 6.3 %collective-permute-done.14 = bf16[192,384]{1,0:T(8,128)(2,1)S(1)} collective-permute-done((bf16[192,384]{1,0:T(8,128)(2,1)S(1)}, bf16[192,384]{1,0:T(8,128)(2,1)S(1)}, u32[]{:S(2)}, u32[]{:S(2)}) %collective-permute-start.14) | collective-permute-done | bytes 147488 | tf_op jit(solution)/shard_map/ppermute | solution.py:601
  167.0 0.6 slice.68
  167.6 0.7 slice.67
  (62 shorter events, 0.6 us)
Async XLA Ops:
  2.2 6.1 %collective-permute-start = (bf16[32,1280]{1,0:T(8,128)(2,1)S(1)}, bf16[32,1280]{1,0:T(8,128)(2,1)S(1)}, u32[]{:S(2)}, u32[]{:S(2)}) collective-permute-start(bf16[32,1280]{1,0:T(8,128)(2,1)S(1)} %pad_maximum_fusion), channel_id=1, source_target_pairs={{0,1},{1,2},{2,3},{3,4},{4,5},{5,6},{6,7},{7,8},{8,9},{9,10},{10,1... | collective-permute-start | bytes 245768 | tf_op jit(solution)/shard_map/ppermute | solution.py:601
  8.3 1.7 copy-start
  9.9 1.2 copy-start.2
  11.2 0.9 copy-start.4
  12.1 0.9 copy-start.5
  13.0 10.2 %copy-start.17 = (f32[1,128,64]{1,2,0:T(8,128)S(1)}, f32[1,128,64]{1,2,0:T(8,128)}, u32[]{:S(2)}) copy-start(f32[1,128,64]{1,2,0:T(8,128)} %param.11) | copy-start | bytes 98308
  14.4 9.7 %copy-start.18 = (f32[1,128,64]{1,2,0:T(8,128)S(1)}, f32[1,128,64]{1,2,0:T(8,128)}, u32[]{:S(2)}) copy-start(f32[1,128,64]{1,2,0:T(8,128)} %param.12) | copy-start | bytes 98308
  14.4 19.9 %collective-permute-start.5 = (bf16[128,1280]{1,0:T(8,128)(2,1)S(1)}, bf16[128,1280]{1,0:T(8,128)(2,1)S(1)}, u32[]{:S(2)}, u32[]{:S(2)}) collective-permute-start(bf16[128,1280]{1,0:T(8,128)(2,1)S(1)} %constant_dynamic-update-slice_fusion), channel_id=1, source_target_pairs={{0,1},{1,0},{2,3},{3,2},{4,5},{5,4},{6,7},{7,6},{8,9},{9,8},{10,11... | collective-permute-start | bytes 983048 | tf_op jit(solution)/shard_map/ppermute | solution.py:605
  15.3 17.9 %all-to-all-start = ((bf16[16,8,1280]{2,1,0:T(8,128)(2,1)}), bf16[16,8,1280]{2,1,0:T(8,128)(2,1)S(1)}, u32[]{:S(2)}, u32[]{:S(2)}) async-start(bf16[16,8,1280]{2,1,0:T(8,128)(2,1)} %broadcast_in_dim.30), calls=%async_computation | async-start | bytes 655360 | tf_op jit(solution)/shard_map/all_to_all | solution.py:611
  25.0 10.4 %collective-permute-start.3 = (bf16[128,1280]{1,0:T(8,128)(2,1)S(1)}, bf16[128,1280]{1,0:T(8,128)(2,1)S(1)}, u32[]{:S(2)}, u32[]{:S(2)}) collective-permute-start(bf16[128,1280]{1,0:T(8,128)(2,1)S(1)} %constant_dynamic-update-slice_fusion), channel_id=1, source_target_pairs={{0,2},{1,3},{2,4},{3,5},{4,6},{5,7},{6,8},{7,9},{8,10},{9,11},{10,... | collective-permute-start | bytes 983048 | tf_op jit(solution)/shard_map/ppermute | solution.py:601
  28.8 13.7 %collective-permute-start.1 = (bf16[128,1280]{1,0:T(8,128)(2,1)S(1)}, bf16[128,1280]{1,0:T(8,128)(2,1)S(1)}, u32[]{:S(2)}, u32[]{:S(2)}) collective-permute-start(bf16[128,1280]{1,0:T(8,128)(2,1)S(1)} %constant_dynamic-update-slice_fusion), channel_id=1, source_target_pairs={{0,4},{1,5},{2,6},{3,7},{4,8},{5,9},{6,10},{7,11},{8,12},{9,13},{1... | collective-permute-start | bytes 983048 | tf_op jit(solution)/shard_map/ppermute | solution.py:601
  33.1 5.1 %copy-start.11 = (bf16[16,8,1280]{2,1,0:T(8,128)(2,1)}, bf16[16,8,1280]{2,1,0:T(8,128)(2,1)S(1)}, u32[]{:S(2)}) copy-start(bf16[16,8,1280]{2,1,0:T(8,128)(2,1)S(1)} %all-to-all-done) | copy-start | bytes 983044
  33.1 10.9 %collective-permute-start.6 = (bf16[128,1280]{1,0:T(8,128)(2,1)S(1)}, bf16[128,1280]{1,0:T(8,128)(2,1)S(1)}, u32[]{:S(2)}, u32[]{:S(2)}) collective-permute-start(bf16[128,1280]{1,0:T(8,128)(2,1)S(1)} %bitcast.71), channel_id=1, source_target_pairs={{0,1},{1,0},{2,3},{3,2},{4,5},{5,4},{6,7},{7,6},{8,9},{9,8},{10,11... | collective-permute-start | bytes 983048 | tf_op jit(solution)/shard_map/ppermute | solution.py:605
  34.4 3.9 %copy-start.8 = (bf16[128,1280]{1,0:T(8,128)(2,1)}, bf16[128,1280]{1,0:T(8,128)(2,1)S(1)}, u32[]{:S(2)}) copy-start(bf16[128,1280]{1,0:T(8,128)(2,1)S(1)} %collective-permute-done.5.mate) | copy-start | bytes 983044
  35.4 8.6 %copy-start.13 = (bf16[128,1280]{1,0:T(8,128)(2,1)}, bf16[128,1280]{1,0:T(8,128)(2,1)S(1)}, u32[]{:S(2)}) copy-start(bf16[128,1280]{1,0:T(8,128)(2,1)S(1)} %collective-permute-done.3.two) | copy-start | bytes 983044
  35.4 23.7 %collective-permute-start.4 = (bf16[128,1280]{1,0:T(8,128)(2,1)S(1)}, bf16[128,1280]{1,0:T(8,128)(2,1)S(1)}, u32[]{:S(2)}, u32[]{:S(2)}) collective-permute-start(bf16[128,1280]{1,0:T(8,128)(2,1)S(1)} %collective-permute-done.3.two), channel_id=1, source_target_pairs={{0,1},{1,0},{2,3},{3,2},{4,5},{5,4},{6,7},{7,6},{8,9},{9,8},{10,11... | collective-permute-start | bytes 983048 | tf_op jit(solution)/shard_map/ppermute | solution.py:605
  42.5 16.5 %copy-start.14 = (bf16[128,1280]{1,0:T(8,128)(2,1)}, bf16[128,1280]{1,0:T(8,128)(2,1)S(1)}, u32[]{:S(2)}) copy-start(bf16[128,1280]{1,0:T(8,128)(2,1)S(1)} %collective-permute-done.1.four) | copy-start | bytes 983044
  42.5 16.7 %collective-permute-start.2 = (bf16[128,1280]{1,0:T(8,128)(2,1)S(1)}, bf16[128,1280]{1,0:T(8,128)(2,1)S(1)}, u32[]{:S(2)}, u32[]{:S(2)}) collective-permute-start(bf16[128,1280]{1,0:T(8,128)(2,1)S(1)} %collective-permute-done.1.four), channel_id=1, source_target_pairs={{0,1},{1,0},{2,3},{3,2},{4,5},{5,4},{6,7},{7,6},{8,9},{9,8},{10,11... | collective-permute-start | bytes 983048 | tf_op jit(solution)/shard_map/ppermute | solution.py:605
  44.0 0.7 copy-start.22
  59.0 33.1 %collective-permute-start.11 = (bf16[128,1280]{1,0:T(8,128)(2,1)}, bf16[128,1280]{1,0:T(8,128)(2,1)S(1)}, u32[]{:S(2)}, u32[]{:S(2)}) collective-permute-start(bf16[128,1280]{1,0:T(8,128)(2,1)} %get-tuple-element.51), channel_id=1, source_target_pairs={{0,1},{1,0},{2,3},{3,2},{4,5},{5,4},{6,7},{7,6},{8,9},{9,8},{10,11... | collective-permute-start | bytes 983048 | tf_op jit(solution)/shard_map/ppermute | solution.py:605
  59.1 0.8 copy-start.15
  59.1 0.9 copy-start.16
  75.7 16.5 %copy-start.12 = (bf16[128,1280]{1,0:T(8,128)(2,1)S(1)}, bf16[128,1280]{1,0:T(8,128)(2,1)}, u32[]{:S(2)}) copy-start(bf16[128,1280]{1,0:T(8,128)(2,1)} %get-tuple-element.52) | copy-start | bytes 983044
  91.3 10.4 %collective-permute-start.7 = (bf16[128,1280]{1,0:T(8,128)(2,1)}, bf16[128,1280]{1,0:T(8,128)(2,1)S(1)}, u32[]{:S(2)}, u32[]{:S(2)}) collective-permute-start(bf16[128,1280]{1,0:T(8,128)(2,1)} %get-tuple-element.47), channel_id=1, source_target_pairs={{0,1},{1,0},{2,3},{3,2},{4,5},{5,4},{6,7},{7,6},{8,9},{9,8},{10,11... | collective-permute-start | bytes 983048 | tf_op jit(solution)/shard_map/ppermute | solution.py:605
  92.1 9.7 %collective-permute-start.8 = (bf16[128,1280]{1,0:T(8,128)(2,1)}, bf16[128,1280]{1,0:T(8,128)(2,1)S(1)}, u32[]{:S(2)}, u32[]{:S(2)}) collective-permute-start(bf16[128,1280]{1,0:T(8,128)(2,1)} %get-tuple-element.49), channel_id=1, source_target_pairs={{0,1},{1,0},{2,3},{3,2},{4,5},{5,4},{6,7},{7,6},{8,9},{9,8},{10,11... | collective-permute-start | bytes 983048 | tf_op jit(solution)/shard_map/ppermute | solution.py:605
  92.2 9.6 %copy-start.9 = (bf16[128,1280]{1,0:T(8,128)(2,1)S(1)}, bf16[128,1280]{1,0:T(8,128)(2,1)}, u32[]{:S(2)}) copy-start(bf16[128,1280]{1,0:T(8,128)(2,1)} %get-tuple-element.50) | copy-start | bytes 983044
  92.2 9.6 %copy-start.10 = (bf16[128,1280]{1,0:T(8,128)(2,1)S(1)}, bf16[128,1280]{1,0:T(8,128)(2,1)}, u32[]{:S(2)}) copy-start(bf16[128,1280]{1,0:T(8,128)(2,1)} %get-tuple-element.48) | copy-start | bytes 983044
  93.3 12.1 %copy-start.19 = (f32[4,8,256]{2,1,0:T(8,128)S(1)}, f32[4,8,256]{2,1,0:T(8,128)}, u32[]{:S(2)}) copy-start(f32[4,8,256]{2,1,0:T(8,128)} %get-tuple-element.54) | copy-start | bytes 98308
  93.3 13.0 %copy-start.20 = (f32[2,8,256]{2,1,0:T(8,128)S(1)}, f32[2,8,256]{2,1,0:T(8,128)}, u32[]{:S(2)}) copy-start(f32[2,8,256]{2,1,0:T(8,128)} %get-tuple-element.55) | copy-start | bytes 49156
  93.3 13.0 %copy-start.21 = (f32[2,8,256]{2,1,0:T(8,128)S(1)}, f32[2,8,256]{2,1,0:T(8,128)}, u32[]{:S(2)}) copy-start(f32[2,8,256]{2,1,0:T(8,128)} %get-tuple-element.56) | copy-start | bytes 49156
  93.3 23.7 %all-to-all-start.1 = ((bf16[16,24,1280]{2,1,0:T(8,128)(2,1)}), bf16[16,24,1280]{2,1,0:T(8,128)(2,1)S(1)}, u32[]{:S(2)}, u32[]{:S(2)}) async-start(bf16[16,24,1280]{2,1,0:T(8,128)(2,1)} %maximum_maximum_fusion), calls=%async_computation.1 | async-start | bytes 1966080 | tf_op jit(solution)/shard_map/all_to_all | solution.py:611
  101.7 15.4 %copy-start.7 = (bf16[128,1280]{1,0:T(8,128)(2,1)}, bf16[128,1280]{1,0:T(8,128)(2,1)S(1)}, u32[]{:S(2)}) copy-start(bf16[128,1280]{1,0:T(8,128)(2,1)S(1)} %collective-permute-done.7) | copy-start | bytes 983044
  102.8 26.8 %collective-permute-start.9 = (bf16[128,1280]{1,0:T(8,128)(2,1)}, bf16[128,1280]{1,0:T(8,128)(2,1)}, u32[]{:S(2)}, u32[]{:S(2)}) collective-permute-start(bf16[128,1280]{1,0:T(8,128)(2,1)} %get-tuple-element.64), channel_id=1, source_target_pairs={{2,0},{3,1},{4,2},{5,3},{6,4},{7,5},{8,6},{9,7},{10,8},{11,9},{12,... | collective-permute-start | bytes 983048 | tf_op jit(solution)/shard_map/ppermute | solution.py:601
  104.1 25.5 %collective-permute-start.10 = (bf16[128,1280]{1,0:T(8,128)(2,1)}, bf16[128,1280]{1,0:T(8,128)(2,1)}, u32[]{:S(2)}, u32[]{:S(2)}) collective-permute-start(bf16[128,1280]{1,0:T(8,128)(2,1)} %get-tuple-element.65), channel_id=1, source_target_pairs={{4,0},{5,1},{6,2},{7,3},{8,4},{9,5},{10,6},{11,7},{12,8},{13,9},{1... | collective-permute-start | bytes 983048 | tf_op jit(solution)/shard_map/ppermute | solution.py:601
  117.9 31.7 %copy-start.1 = (bf16[6144,192]{0,1:T(8,128)(2,1)S(1)}, bf16[6144,192]{0,1:T(8,128)(2,1)}, u32[]{:S(2)}) copy-start(bf16[6144,192]{0,1:T(8,128)(2,1)} %param.14) | copy-start | bytes 7077892
  117.9 31.7 %copy-start.6 = (s32[2]{0:T(128)S(1)}, s32[2]{0:T(128)}, u32[]{:S(2)}) copy-start(s32[2]{0:T(128)} %pad_add_fusion.place_ref) | copy-start | bytes 28
  117.9 19.2 %all-to-all-start.2 = ((bf16[16,8,1280]{2,1,0:T(8,128)(2,1)}), bf16[16,8,1280]{2,1,0:T(8,128)(2,1)}, u32[]{:S(2)}, u32[]{:S(2)}) async-start(bf16[16,8,1280]{2,1,0:T(8,128)(2,1)} %broadcast_in_dim.34), calls=%async_computation.2 | async-start | bytes 655360 | tf_op jit(solution)/shard_map/all_to_all | solution.py:611
  137.0 12.5 %collective-permute-start.12 = (bf16[128,1280]{1,0:T(8,128)(2,1)}, bf16[128,1280]{1,0:T(8,128)(2,1)S(1)}, u32[]{:S(2)}, u32[]{:S(2)}) collective-permute-start(bf16[128,1280]{1,0:T(8,128)(2,1)} %bitcast.19.mine_ref), channel_id=1, source_target_pairs={{0,1},{1,0},{2,3},{3,2},{4,5},{5,4},{6,7},{7,6},{8,9},{9,8},{10,11... | collective-permute-start | bytes 983048 | tf_op jit(solution)/shard_map/ppermute | solution.py:605
  149.6 1.2 copy-start.3
  153.6 7.0 %collective-permute-start.15 = (bf16[192,384]{1,0:T(8,128)(2,1)S(1)}, bf16[192,384]{1,0:T(8,128)(2,1)S(1)}, u32[]{:S(2)}, u32[]{:S(2)}) collective-permute-start(bf16[192,384]{1,0:T(8,128)(2,1)S(1)} %get-tuple-element.57), channel_id=1, source_target_pairs={{0,96},{32,0},{64,32},{96,64},{1,97},{33,1},{65,33},{97,65},{2,98}... | collective-permute-start | bytes 442376 | tf_op jit(solution)/shard_map/ppermute | solution.py:601
  157.4 9.5 %collective-permute-start.14 = (bf16[192,384]{1,0:T(8,128)(2,1)S(1)}, bf16[192,384]{1,0:T(8,128)(2,1)S(1)}, u32[]{:S(2)}, u32[]{:S(2)}) collective-permute-start(bf16[192,384]{1,0:T(8,128)(2,1)S(1)} %get-tuple-element.57), channel_id=1, source_target_pairs={{0,32},{32,64},{64,96},{96,0},{1,33},{33,65},{65,97},{97,1},{2,34}... | collective-permute-start | bytes 442376 | tf_op jit(solution)/shard_map/ppermute | solution.py:601
  157.4 9.5 %collective-permute-start.13 = (bf16[192,384]{1,0:T(8,128)(2,1)S(1)}, bf16[192,384]{1,0:T(8,128)(2,1)S(1)}, u32[]{:S(2)}, u32[]{:S(2)}) collective-permute-start(bf16[192,384]{1,0:T(8,128)(2,1)S(1)} %get-tuple-element.57), channel_id=1, source_target_pairs={{0,64},{32,96},{64,0},{96,32},{1,65},{33,97},{65,1},{97,33},{2,66}... | collective-permute-start | bytes 442376 | tf_op jit(solution)/shard_map/ppermute | solution.py:601

commit v2 on v1

--- a/solution.py
+++ b/solution.py
@@ -442,22 +442,117 @@
     return jnp.concatenate([left[:, :128], left[:, 128:] + right[:, :128], right[:, 128:]], axis=1)
 
 
-def compress_kernel(k_ref, v_ref, prior_ref, wk_ref, wv_ref, out_ref, ext, y_scr, *, dh, dv, groups):
+def pack_kernel(k_ref, v_ref, own_ref, last_ref):
     tokens, kw = k_ref.shape
+    own_ref[:, :kw] = k_ref[...]
+    own_ref[:, kw:] = v_ref[...]
+    last_ref[:, :kw] = k_ref[tokens - BLK :, :]
+    last_ref[:, kw:] = v_ref[tokens - BLK :, :]
+
+
+def pack(keys, values):
+    tokens, both = keys.shape[0], keys.shape[1] + values.shape[1]
+    return pl.pallas_call(
+        pack_kernel,
+        out_shape=[jax.ShapeDtypeStruct((n, both), keys.dtype) for n in (tokens, BLK)],
+        compiler_params=pltpu.CompilerParams(vmem_limit_bytes=56 * 2**20),
+        name="pack",
+    )(keys, values)
+
+
+def fold_kernel(place_ref, mine_ref, other_ref, rows_ref, mate_ref, out_ref):
+    chips = out_ref.shape[0]
+    blocks = mine_ref.shape[0] // chips
+    total = mine_ref[...].astype(jnp.float32) + other_ref[...].astype(jnp.float32)
+    rows, mate = rows_ref[...].astype(jnp.float32), mate_ref[...].astype(jnp.float32)
+    core = place_ref[1]
+    one, two = jnp.where(core == 0, rows, mate), jnp.where(core == 0, mate, rows)
+    for chip in range(chips):
+        at = slice(chip * blocks, (chip + 1) * blocks)
+        of = slice(chip * blocks % rows.shape[0], chip * blocks % rows.shape[0] + blocks)
+        out_ref[chip] = jnp.concatenate([total[at], one[of], two[of]], axis=0).astype(jnp.bfloat16)
+
+
+def fold(place, mine, other, rows, mate, chips):
+    vmem = pl.BlockSpec(memory_space=pltpu.VMEM)
+    return pl.pallas_call(
+        fold_kernel,
+        in_specs=[pl.BlockSpec(memory_space=pltpu.SMEM), vmem, vmem, vmem, vmem],
+        out_shape=jax.ShapeDtypeStruct((chips, 3 * mine.shape[0] // chips, mine.shape[1]), mine.dtype),
+        compiler_params=pltpu.CompilerParams(vmem_limit_bytes=56 * 2**20),
+        name="fold",
+    )(place, mine, other, rows, mate)
+
+
+def pass_kernel(place_ref, four_ref, two_ref, near_ref, nearest_ref, to_four_ref, to_two_ref):
+    core = place_ref[1]
+    near, nearest = near_ref[...].astype(jnp.float32), nearest_ref[...].astype(jnp.float32)
+    to_four_ref[...] = (four_ref[...].astype(jnp.float32) + jnp.where(core == 0, 0.0, near)).astype(jnp.bfloat16)
+    to_two_ref[...] = (two_ref[...].astype(jnp.float32) + jnp.where(core == 0, near, nearest)).astype(jnp.bfloat16)
+
+
+def pass_on(place, *arrays):
+    vmem = pl.BlockSpec(memory_space=pltpu.VMEM)
+    return pl.pallas_call(
+        pass_kernel,
+        in_specs=[pl.BlockSpec(memory_space=pltpu.SMEM), *[vmem] * 4],
+        out_shape=[jax.ShapeDtypeStruct(arrays[0].shape, jnp.bfloat16)] * 2,
+        compiler_params=pltpu.CompilerParams(vmem_limit_bytes=56 * 2**20),
+        name="pass_on",
+    )(place, *arrays)
+
+
+def final_kernel(place_ref, keep_ref, nearest_ref, two_ref, four_ref, back_ref, gk_ref, gv_ref, *, kspan, vspan):
+    core = place_ref[1]
+    pairs = gk_ref.shape[1] // kspan
+    for pair in range(pairs):
+        for ref, at, to, of, width in (
+            (gk_ref, 0, pair * kspan, pair * kspan, kspan),
+            (gv_ref, kspan, pair * vspan, pairs * kspan + pair * vspan, vspan),
+        ):
+            lanes = slice(pair * (kspan + vspan) + at, pair * (kspan + vspan) + at + width)
+            total = keep_ref[:, lanes] + jnp.where(core == 0, nearest_ref[:, lanes].astype(jnp.float32), 0.0)
+            total = total + two_ref[:, lanes].astype(jnp.float32) + four_ref[:, lanes].astype(jnp.float32)
+            ref[:, to : to + width] = (total + back_ref[:, of : of + width]).astype(jnp.bfloat16)
+
+
+def final(place, keep, nearest, two, four, back, groups, dh, dv):
+    vmem = pl.BlockSpec(memory_space=pltpu.VMEM)
+    tokens = keep.shape[0]
+    return pl.pallas_call(
+        functools.partial(final_kernel, kspan=2 * dh, vspan=2 * dv),
+        in_specs=[pl.BlockSpec(memory_space=pltpu.SMEM), *[vmem] * 5],
+        out_shape=[jax.ShapeDtypeStruct((tokens, groups * d), jnp.bfloat16) for d in (dh, dv)],
+        compiler_params=pltpu.CompilerParams(vmem_limit_bytes=16 * 2**20),
+        name="final",
+    )(place, keep, nearest, two, four, back)
+
+
+def compress_kernel(place_ref, own_ref, prior_ref, wk_ref, wv_ref, out_ref, rows_ref, mates_ref, ext, y_scr, acc_k, acc_v, *, dh, dv, groups, offsets):
+    tokens, _ = own_ref.shape
+    kw = groups * dh
     tiles = ext.shape[0]
-    for n in range(tiles):
-        at = n * 128
-        ext[n, :BLK, :] = prior_ref[:, at : at + 128].astype(jnp.float32)
-        ref, at = (k_ref, at) if at < kw else (v_ref, at - kw)
-        ext[n, BLK:, :] = ref[:, at : at + 128].astype(jnp.float32)
+    blocks = tokens // STRIDE
+    step = pl.program_id(0)
+
+    @pl.when(step == 0)
+    def _():
+        for n in range(tiles):
+            lanes = slice(n * 128, n * 128 + 128)
+            ext[n, :BLK, :] = prior_ref[:, lanes].astype(jnp.float32)
+            ext[n, BLK:, :] = own_ref[:, lanes].astype(jnp.float32)
+        acc_k[...] = jnp.zeros_like(acc_k)
+        acc_v[...] = jnp.zeros_like(acc_v)
+        for ref, odd in ((rows_ref, place_ref[1]), (mates_ref, 1 - place_ref[1])):
+            for n in range(tiles):
+                rows = [ext[n, pl.ds(BLK + at + odd, blocks, stride=STRIDE), :] for at in range(0, STRIDE, 2)]
+                ref[:, n * 128 : n * 128 + 128] = jnp.concatenate(rows, axis=0).astype(jnp.bfloat16)
 
     def every(p):
-        return jnp.concatenate([ext[n, pl.ds(p, blocks, stride=STRIDE), :] for n in range(tiles)], axis=1)
-
-    blocks = tokens // STRIDE
-    acc_k = jnp.zeros((groups * blocks, dh), jnp.float32)
-    acc_v = jnp.zeros((groups * blocks, dv), jnp.float32)
-    for p in range(0, BLK, 2):
+        return jnp.concatenate([ext[n, pl.ds(step * offsets + p, blocks, stride=STRIDE), :] for n in range(tiles)], axis=1)
+
+    sum_k, sum_v = acc_k[...], acc_v[...]
+    for p in range(0, offsets, 2):
         one, two = every(p), every(p + 1)
         rows = []
         for g in range(groups):
@@ -469,35 +564,60 @@
                 left = to_left(split_lanes(one[:, at : at + 2 * dh], dh, True), dh)
                 right = split_lanes(two[:, at : at + 2 * dh], dh, True)
             rows.append(joined(left, right))
-        acc_k += nt(jnp.concatenate(rows, axis=0).astype(jnp.bfloat16), wk_ref[:, p * dh : (p + 2) * dh])
+        sum_k += nt(jnp.concatenate(rows, axis=0).astype(jnp.bfloat16), wk_ref[:, p * dh : (p + 2) * dh])
         vals = [
             jnp.concatenate([x[:, kw + g * dv : kw + (g + 1) * dv] for x in (one, two)], axis=1) for g in range(groups)
         ]
-        acc_v += nn(jnp.concatenate(vals, axis=0).astype(jnp.bfloat16), wv_ref[p * dv : (p + 2) * dv, :])
-    y_scr[...] = jnp.zeros_like(y_scr)
-    y_scr[:, :dh] = acc_k
-    for m in range(groups // 2):
-        left = y_scr[2 * m * blocks : (2 * m + 1) * blocks, :]
-        right = to_right(y_scr[(2 * m + 1) * blocks : (2 * m + 2) * blocks, :], dh)
-        out_ref[:, 2 * m * dh : 2 * (m + 1) * dh] = joined(left, right).astype(jnp.bfloat16)
-    for g in range(groups):
-        out_ref[:, kw + g * dv : kw + (g + 1) * dv] = acc_v[g * blocks : (g + 1) * blocks].astype(jnp.bfloat16)
-
-
-def compress(keys, values, prior, wk_t, wv, groups):
+        sum_v += nn(jnp.concatenate(vals, axis=0).astype(jnp.bfloat16), wv_ref[p * dv : (p + 2) * dv, :])
+    acc_k[...] = sum_k
+    acc_v[...] = sum_v
+
+    @pl.when(step == pl.num_programs(0) - 1)
+    def _():
+        y_scr[...] = jnp.zeros_like(y_scr)
+        y_scr[:, :dh] = acc_k[...]
+        outs = []
+        for m in range(groups // 2):
+            left = y_scr[2 * m * blocks : (2 * m + 1) * blocks, :]
+            right = to_right(y_scr[(2 * m + 1) * blocks : (2 * m + 2) * blocks, :], dh)
+            outs.append(joined(left, right))
+        outs += [acc_v[g * blocks : (g + 1) * blocks, :] for g in range(groups)]
+        out = jnp.concatenate(outs, axis=1).astype(jnp.bfloat16)
+        for n in range(out_ref.shape[0]):
+            out_ref[n] = out
+
+
+def compress(place, own, prior, wk_t, wv, groups, copies):
     dh, dv = wk_t.shape[0], wv.shape[1]
-    blocks = keys.shape[0] // STRIDE
-    both = keys.shape[1] + values.shape[1]
+    blocks, both = own.shape[0] // STRIDE, own.shape[1]
+    steps = 2
+    offsets = BLK // steps
+    whole = lambda shape: pl.BlockSpec(shape, lambda i: (0,) * len(shape))
+    in_hbm = lambda x: pltpu.with_memory_space_constraint(x, pltpu.HBM)
     return pl.pallas_call(
-        functools.partial(compress_kernel, dh=dh, dv=dv, groups=groups),
-        out_shape=jax.ShapeDtypeStruct((blocks, both), jnp.bfloat16),
+        functools.partial(compress_kernel, dh=dh, dv=dv, groups=groups, offsets=offsets),
+        grid=(steps,),
+        in_specs=[
+            pl.BlockSpec(memory_space=pltpu.SMEM),
+            whole(own.shape),
+            whole(prior.shape),
+            pl.BlockSpec((dh, offsets * dh), lambda i: (0, i)),
+            pl.BlockSpec((offsets * dv, dv), lambda i: (i, 0)),
+        ],
+        out_specs=[whole((copies, blocks, both)), *[whole((STRIDE // 2 * blocks, both))] * 2],
+        out_shape=[
+            jax.ShapeDtypeStruct((copies, blocks, both), jnp.bfloat16),
+            *[jax.ShapeDtypeStruct((STRIDE // 2 * blocks, both), jnp.bfloat16)] * 2,
+        ],
         scratch_shapes=[
-            pltpu.VMEM((both // 128, BLK + keys.shape[0], 128), jnp.float32),
+            pltpu.VMEM((both // 128, BLK + own.shape[0], 128), jnp.float32),
             pltpu.VMEM((groups * blocks, 256), jnp.float32),
-        ],
-        compiler_params=pltpu.CompilerParams(vmem_limit_bytes=40 * 2**20),
+            pltpu.VMEM((groups * blocks, dh), jnp.float32),
+            pltpu.VMEM((groups * blocks, dv), jnp.float32),
+        ],
+        compiler_params=pltpu.CompilerParams(dimension_semantics=("arbitrary",), vmem_limit_bytes=56 * 2**20),
         name="compress",
-    )(keys, values, prior, wk_t, wv)
+    )(place, own, prior, in_hbm(wk_t), in_hbm(wv))
 
 
 def back_kernel(place_ref, mine_ref, other_ref, got_ref, wk_ref, wv_ref, part_ref, back_ref, wide, spread, *, dh, dv, groups):
@@ -575,7 +695,7 @@
             pltpu.VMEM((2 * half + 16, both), jnp.float32),
             pltpu.VMEM((both // 128, tokens, 128), jnp.float32),
         ],
-        compiler_params=pltpu.CompilerParams(vmem_limit_bytes=40 * 2**20),
+        compiler_params=pltpu.CompilerParams(vmem_limit_bytes=16 * 2**20),
         name="compress_back",
     )(place, mine, other, got, wk_t, wv)
 
@@ -611,9 +731,8 @@
     return lax.all_to_all(array, "seq", 0, 0, axis_index_groups=rings, tiled=True)
 
 
-def gathered(array):
-    chips = lax.axis_size("seq") // 2
-    mine = between_chips(jnp.broadcast_to(array[None], (chips, *array.shape))).reshape(-1, array.shape[1])
+def gathered(copies):
+    mine = between_chips(copies).reshape(-1, copies.shape[2])
     return mine, to_sibling(mine)
 
 
@@ -627,32 +746,26 @@
     core = shard % 2
     place = jnp.stack([shard, core])
     wk_t = compress_key.T
-    last = jnp.concatenate([keys[tokens - BLK :], values[tokens - BLK :]], axis=1)
+    own, last = pack(keys, values)
     prior = shifted(last, "seq", 1)
-    cmp_own = compress(keys, values, prior, wk_t, compress_value, groups)
+    cmp_own, rows, mate_rows = compress(place, own, prior, wk_t, compress_value, groups, shards // 2)
     mine, other = gathered(cmp_own)
-    late_keys, late_values, _ = lax.optimization_barrier((keys, values, cmp_own))
-    own = jnp.concatenate([late_keys, late_values], axis=1)
-    both = own.shape[1]
     two = shifted(own, "seq", 2)
     four = shifted(own, "seq", 4)
     mate = to_sibling(own)
     two_mate = to_sibling(two)
     four_mate = to_sibling(four)
+    mate_rows = to_sibling(mate_rows)
+    gates = [gate_rows(x, groups) for x in lax.optimization_barrier((gate_cmp[0], gate_win[0], cmp_own))[:2]]
     halos = [four, four_mate, two, two_mate, mate]
-    oc, dqc, ggc, gmine, gother = attend_cmp(place, q, c, gate_rows(gate_cmp[0], groups), mine, other, groups, dh, dv)
-    chip = jnp.where(core == 0, jnp.stack([own, mate]), jnp.stack([mate, own]))
-    chip = chip.reshape(2 * tokens // STRIDE, STRIDE // 2, 2, both)
-    residue = jnp.where(core == 0, chip[:, :, 0], chip[:, :, 1]).transpose(1, 0, 2)
-    residue = jnp.concatenate([residue, residue], axis=0)
+    oc, dqc, ggc, gmine, gother = attend_cmp(place, q, c, gates[0], mine, other, groups, dh, dv)
+    blocks_dev = cmp_own.shape[1]
     folded = to_sibling(gother)
-    blocks_dev = cmp_own.shape[0]
-    folded = (folded.astype(jnp.float32) + gmine.astype(jnp.float32)).astype(jnp.bfloat16)
-    sent = jnp.concatenate([folded.reshape(shards // 2, blocks_dev, both), residue], axis=1)
+    sent = fold(place, gmine, folded, rows, mate_rows, shards // 2)
     got = between_chips(sent)
     gckb = jnp.sum(got[:, :blocks_dev].astype(jnp.float32), axis=0).astype(jnp.bfloat16)
-    grads = gathered(gckb)
-    win = functools.partial(attend_win, place, q, c, gate_rows(gate_win[0], groups), keys, values, halos, oc, dqc, groups, dh, dv)
+    grads = gathered(jnp.broadcast_to(gckb[None], cmp_own.shape))
+    win = functools.partial(attend_win, place, q, c, gates[1], keys, values, halos, oc, dqc, groups, dh, dv)
     ggw, before = [], ()
     for pair in range(groups // 2):
         attended, grad_query, gg, *gk = win(pair, before)
@@ -660,27 +773,22 @@
         before = (attended, grad_query, *gk)
     to_behind4, to_behind3, to_behind2, to_behind1, keep = gk
     near, nearest = to_sibling(to_behind3), to_sibling(to_behind1)
-    near, nearest = near.astype(jnp.float32), nearest.astype(jnp.float32)
-    to_four = (to_behind4.astype(jnp.float32) + jnp.where(core == 0, 0.0, near)).astype(jnp.bfloat16)
-    to_two = (to_behind2.astype(jnp.float32) + jnp.where(core == 0, near, nearest)).astype(jnp.bfloat16)
+    to_four, to_two = pass_on(place, to_behind4, to_behind2, near, nearest)
     from_four, from_two = shifted(to_four, "seq", -4), shifted(to_two, "seq", -2)
-    keep = keep + jnp.where(core == 0, nearest, 0.0)
-    keep = keep + from_two.astype(jnp.float32) + from_four.astype(jnp.float32)
-    half = 2 * (dh + dv)
-    keys_back = jnp.concatenate([keep[:, at : at + 2 * dh] for at in (0, half)], axis=1)
-    values_back = jnp.concatenate([keep[:, at + 2 * dh : at + half] for at in (0, half)], axis=1)
     part, back = compress_back(place, *grads, got, wk_t, compress_value, tokens, groups)
     parts = [shifted(part, "dp", by, True).astype(jnp.float32) for by in (1, 2, 3)]
     total = (part.astype(jnp.float32) + parts[1]) + (parts[0] + parts[2])
-    grad_key = keys_back + back[:, :kw]
-    grad_value = values_back + back[:, kw:]
+    ggc, ggw, part = lax.optimization_barrier((ggc, jnp.concatenate(ggw, axis=0), part))
+    gate_grads = [gate_columns(x, tokens) for x in (ggc, ggw)]
+    total, gate_grads, from_two, from_four = lax.optimization_barrier((total, gate_grads, from_two, from_four))
+    grad_key, grad_value = final(place, keep, nearest, from_two, from_four, back, groups, dh, dv)
     return (
         attended[None],
         grad_query[None],
-        grad_key.astype(jnp.bfloat16)[None],
-        grad_value.astype(jnp.bfloat16)[None],
-        gate_columns(ggc, tokens)[None],
-        gate_columns(jnp.concatenate(ggw, axis=0), tokens)[None],
+        grad_key[None],
+        grad_value[None],
+        gate_grads[0][None],
+        gate_grads[1][None],
         total[:, :dh],
         total[:dv, 256:],
     )

time: 169 us -> 163 us (0.964)
  the two profiles are of different devices: /device:TPU:1 before, /device:TPU:16 now
where the time goes in v2:
time: 163 us; the launch traced here: 162 us
  Pallas kernels  59.5 us (37%)
  waiting for transfers between devices  41.9 us (26%)
  starting transfers between devices  35.5 us (22%)
  blocking collectives  14.1 us (9%)
  local copies, waits for them, and re-layouts  9.36 us (6%)
    ppermute x8, waiting for transfers between devices, shifted(): return lax.ppermute(array, axis, pairs)  39.6 us
    pallas_call x2, Pallas kernels, attend_win(): pl.pallas_call(functools.partial(win_kernel, dh=dh, dv=dv, pair=pair), gr...  31.1 us
    ppermute x8, starting transfers between devices, shifted(): return lax.ppermute(array, axis, pairs)  21 us
    pallas_call x1, Pallas kernels, attend_cmp(): pl.pallas_call(functools.partial(cmp_kernel, dh=dh, dv=dv), grid=(groups,...  14.3 us
    all_to_all x1, blocking collectives, between_chips(): lax.all_to_all(array, 'seq', 0, 0, axis_index_groups=rings, tiled=True)  14.1 us
    all_to_all x2, starting transfers between devices, between_chips(): lax.all_to_all(array, 'seq', 0, 0, axis_index_groups=rings, tiled=True)  12.9 us
    pallas_call x1, Pallas kernels, compress(): pl.pallas_call(functools.partial(compress_kernel, dh=dh, dv=dv, groups=gr...  4.14 us
    unnamed x48, local copies, waits for them, and re-layouts  3.85 us
  transfers between devices with their start and end apart: 19, of which 7 were waited for; matrix products, arithmetic and copies ran while one was open for 3% of the time, Pallas kernels for 22%

profile of v2, /device:TPU:16, one launch (start us, length us, event | category | flops | bytes accessed | tf_op | source)
XLA Modules:
  0.0 162.2 jit_solution(5490737441803630818)
XLA Ops:
  0.6 1.8 %pack.1 = (bf16[128,1280]{1,0:T(8,128)(2,1)}, bf16[32,1280]{1,0:T(8,128)(2,1)}) custom-call(bf16[128,768]{1,0:T(8,128)(2,1)} %bitcast.49, bf16[128,512]{1,0:T(8,128)(2,1)} %bitcast.52), custom_call_target="tpu_custom_call" | custom-call | tf_op jit(solution)/shard_map/pack/pallas_call | solution.py:455
  2.4 1.9 %collective-permute-start = (bf16[32,1280]{1,0:T(8,128)(2,1)}, bf16[32,1280]{1,0:T(8,128)(2,1)S(1)}, u32[]{:S(2)}, u32[]{:S(2)}) collective-permute-start(bf16[32,1280]{1,0:T(8,128)(2,1)} %get-tuple-element.50), channel_id=1, source_target_pairs={{0,1},{1,2},{2,3},{3,4},{4,5},{5,6},{6,7},{7,8},{8,9},{9,10},{10,1... | collective-permute-start | bytes 245768 | tf_op jit(solution)/shard_map/ppermute | solution.py:721
  4.3 0.6 pad_add_fusion.place_ref
  4.9 3.4 %collective-permute-done.prior_ref = bf16[32,1280]{1,0:T(8,128)(2,1)S(1)} collective-permute-done((bf16[32,1280]{1,0:T(8,128)(2,1)}, bf16[32,1280]{1,0:T(8,128)(2,1)S(1)}, u32[]{:S(2)}, u32[]{:S(2)}) %collective-permute-start) | collective-permute-done | bytes 81952 | tf_op jit(solution)/shard_map/ppermute | solution.py:721
  8.4 0.6 copy-done.16
  9.0 4.1 %compress.1 = (bf16[16,8,1280]{2,1,0:T(8,128)(2,1)}, bf16[64,1280]{1,0:T(8,128)(2,1)}, bf16[64,1280]{1,0:T(8,128)(2,1)}) custom-call(s32[2]{0:T(128)} %pad_add_fusion.place_ref, bf16[128,1280]{1,0:T(8,128)(2,1)} %get-tuple-element.49.own_ref, bf16[32,1280]{1,0:T(8,128)(2,1)} %copy-done.16, bf16[192,6144]{1,0:T(8,128)(2,1)} %bitcast.37, bf16[4096,128]{1,0:T(8,128)(2,1)} %wv_ref.3), custom_call_target="tpu_custom_call" | custom-call | tf_op jit(solution)/shard_map/compress/pallas_call | solution.py:597
  13.2 14.1 %all_to_all.15 = bf16[16,8,1280]{2,1,0:T(8,128)(2,1)S(1)} all-to-all(bf16[16,8,1280]{2,1,0:T(8,128)(2,1)} %get-tuple-element.51), channel_id=1, replica_groups={{0,2,4,6,8,10,12,14,16,18,20,22,24,26,28,30},{1,3,5,7,9,11,13,15,17,19,..., dimensions={0} | all-to-all | bytes 655360 | tf_op jit(solution)/shard_map/all_to_all | solution.py:731
  27.3 0.1 reshape.49
  27.4 0.7 reshape.50.gate_ref
  28.2 0.8 collective-permute-done.6.dk_ref.dv_ref
  28.9 0.7 copy-done.22
  29.6 14.3 %attend_cmp.1 = (bf16[4,8,128,256]{3,2,1,0:T(8,128)(2,1)}, bf16[4,4,384,256]{3,2,1,0:T(8,128)(2,1)}, f32[4,8,256]{2,1,0:T(8,128)}, bf16[128,1280]{1,0:T(8,128)(2,1)}, bf16[128,1280]{1,0:T(8,128)(2,1)}) custom-call(s32[2]{0:T(128)} %pad_add_fusion.place_ref, bf16[128,12288]{1,0:T(8,128)(2,1)} %bitcast.41, bf16[128,8192]{1,0:T(8,128)(2,1)} %bitcast.45, ...), custom_call_target="tpu_custom_call" | custom-call | flops 4026531840 | bytes 30000000 | tf_op jit(solution)/shard_map/attend_cmp/pallas_call | solution.py:351
  43.9 0.0 copy-start.10
  43.9 0.0 copy-start.18
  44.0 0.2 collective-permute-start.8
  44.2 0.4 collective-permute-start.9
  44.5 1.6 collective-permute-done.9.mate_ref
  46.1 0.0 collective-permute-done.8.other_ref
  46.1 0.7 copy-done.15
  46.8 0.1 copy-done.9
  46.9 2.2 %fold.1 = bf16[16,24,1280]{2,1,0:T(8,128)(2,1)} custom-call(s32[2]{0:T(128)} %pad_add_fusion.place_ref, bf16[128,1280]{1,0:T(8,128)(2,1)} %get-tuple-element.67.mine_ref, bf16[128,1280]{1,0:T(8,128)(2,1)} %copy-done.9, bf16[64,1280]{1,0:T(8,128)(2,1)} %get-tuple-element.69.rows_ref, bf16[64,1280]{1,0:T(8,128)(2,1)} %copy-done.15), custom_call_target="tpu_custom_call" | custom-call | tf_op jit(solution)/shard_map/fold/pallas_call | solution.py:478
  49.1 5.7 %all-to-all-start.1 = ((bf16[16,24,1280]{2,1,0:T(8,128)(2,1)}), bf16[16,24,1280]{2,1,0:T(8,128)(2,1)S(1)}, u32[]{:S(2)}, u32[]{:S(2)}) async-start(bf16[16,24,1280]{2,1,0:T(8,128)(2,1)} %fold.1), calls=%async_computation.1 | async-start | bytes 1966080 | tf_op jit(solution)/shard_map/all_to_all | solution.py:731
  54.8 3.4 %collective-permute-start.1 = (bf16[128,1280]{1,0:T(8,128)(2,1)S(1)}, bf16[128,1280]{1,0:T(8,128)(2,1)S(1)}, u32[]{:S(2)}, u32[]{:S(2)}) collective-permute-start(bf16[128,1280]{1,0:T(8,128)(2,1)S(1)} %copy-done.10), channel_id=1, source_target_pairs={{0,4},{1,5},{2,6},{3,7},{4,8},{5,9},{6,10},{7,11},{8,12},{9,13},{1... | collective-permute-start | bytes 983048 | tf_op jit(solution)/shard_map/ppermute | solution.py:721
  58.2 4.0 %collective-permute-start.3 = (bf16[128,1280]{1,0:T(8,128)(2,1)S(1)}, bf16[128,1280]{1,0:T(8,128)(2,1)S(1)}, u32[]{:S(2)}, u32[]{:S(2)}) collective-permute-start(bf16[128,1280]{1,0:T(8,128)(2,1)S(1)} %copy-done.10), channel_id=1, source_target_pairs={{0,2},{1,3},{2,4},{3,5},{4,6},{5,7},{6,8},{7,9},{8,10},{9,11},{10,... | collective-permute-start | bytes 983048 | tf_op jit(solution)/shard_map/ppermute | solution.py:721
  62.1 0.1 collective-permute-start.5
  62.2 13.4 %collective-permute-done.1.four = bf16[128,1280]{1,0:T(8,128)(2,1)S(1)} collective-permute-done((bf16[128,1280]{1,0:T(8,128)(2,1)S(1)}, bf16[128,1280]{1,0:T(8,128)(2,1)S(1)}, u32[]{:S(2)}, u32[]{:S(2)}) %collective-permute-start.1) | collective-permute-done | bytes 327712 | tf_op jit(solution)/shard_map/ppermute | solution.py:721
  75.6 0.0 collective-permute-start.2
  75.6 6.3 %collective-permute-done.3.two = bf16[128,1280]{1,0:T(8,128)(2,1)S(1)} collective-permute-done((bf16[128,1280]{1,0:T(8,128)(2,1)S(1)}, bf16[128,1280]{1,0:T(8,128)(2,1)S(1)}, u32[]{:S(2)}, u32[]{:S(2)}) %collective-permute-start.3) | collective-permute-done | bytes 327712 | tf_op jit(solution)/shard_map/ppermute | solution.py:721
  82.0 0.0 collective-permute-start.4
  82.0 0.1 reshape.47
  82.2 0.7 reshape.48.gate_ref
  82.9 0.1 slice_reduce_fusion
  82.9 0.7 broadcast_in_dim.26
  83.7 7.3 %all-to-all-start.2 = ((bf16[16,8,1280]{2,1,0:T(8,128)(2,1)}), bf16[16,8,1280]{2,1,0:T(8,128)(2,1)S(1)}, u32[]{:S(2)}, u32[]{:S(2)}) async-start(bf16[16,8,1280]{2,1,0:T(8,128)(2,1)} %broadcast_in_dim.26), calls=%async_computation.2 | async-start | bytes 655360 | tf_op jit(solution)/shard_map/all_to_all | solution.py:731
  91.0 0.7 copy-done.13
  91.7 0.1 copy-done.14
  91.8 15.5 %attend_win.2 = (bf16[128,8192]{1,0:T(8,128)(2,1)}, bf16[128,12288]{1,0:T(8,128)(2,1)}, f32[2,8,256]{2,1,0:T(8,128)}, bf16[128,1280]{1,0:T(8,128)(2,1)}, bf16[12...) custom-call(s32[2]{0:T(128)} %pad_add_fusion.place_ref, ...), custom_call_target="tpu_custom_call" | custom-call | flops 5033164800 | bytes 30000000 | tf_op jit(solution)/shard_map/attend_win/pallas_call | solution.py:390
  107.3 0.3 collective-permute-start.10
  107.6 0.0 copy-start
  107.6 0.0 copy-start.1
  107.6 15.7 %attend_win.3 = (bf16[128,8192]{1,0:T(8,128)(2,1)}, bf16[128,12288]{1,0:T(8,128)(2,1)}, f32[2,8,256]{2,1,0:T(8,128)}, bf16[128,1280]{1,0:T(8,128)(2,1)}, bf16[12...) custom-call(s32[2]{0:T(128)} %pad_add_fusion.place_ref, ...), custom_call_target="tpu_custom_call", output_to_operand_aliasing={{0}: (13, {}), {1}: (14, {}), {3}: (15, {}), {4}: (16, {}),... | custom-call | flops 5033164800 | bytes 30000000 | tf_op jit(solution)/shard_map/attend_win/pallas_call | solution.py:390
  123.3 0.5 collective-permute-start.14
  123.9 0.1 collective-permute-start.7
  124.0 2.3 %compress_back.1 = (bf16[192,384]{1,0:T(8,128)(2,1)S(1)}, f32[128,1280]{1,0:T(8,128)S(1)}) custom-call(s32[2]{0:T(128)S(1)} %copy-done.5, bf16[128,1280]{1,0:T(8,128)(2,1)S(1)} %bitcast.40, bf16[128,1280]{1,0:T(8,128)(2,1)S(1)} %collective-permute-done.10.other_ref, bf16[16,24,1280]{2,1,0:T(8,128)(2,1)S(1)} %all-to-all-done.1.got_ref, ...), custom_call_target="tpu_custom_call" | custom-call | tf_op jit(solution)/shard_map/compress_back/pallas_call | solution.py:687
  126.3 4.0 %collective-permute-start.11 = (bf16[192,384]{1,0:T(8,128)(2,1)S(1)}, bf16[192,384]{1,0:T(8,128)(2,1)S(1)}, u32[]{:S(2)}, u32[]{:S(2)}) collective-permute-start(bf16[192,384]{1,0:T(8,128)(2,1)S(1)} %get-tuple-element.71), channel_id=1, source_target_pairs={{0,64},{32,96},{64,0},{96,32},{1,65},{33,97},{65,1},{97,33},{2,66}... | collective-permute-start | bytes 442376 | tf_op jit(solution)/shard_map/ppermute | solution.py:721
  130.3 1.0 collective-permute-start.12
  131.3 2.2 %collective-permute-start.13 = (bf16[192,384]{1,0:T(8,128)(2,1)S(1)}, bf16[192,384]{1,0:T(8,128)(2,1)S(1)}, u32[]{:S(2)}, u32[]{:S(2)}) collective-permute-start(bf16[192,384]{1,0:T(8,128)(2,1)S(1)} %get-tuple-element.71), channel_id=1, source_target_pairs={{0,96},{32,0},{64,32},{96,64},{1,97},{33,1},{65,33},{97,65},{2,98}... | collective-permute-start | bytes 442376 | tf_op jit(solution)/shard_map/ppermute | solution.py:721
  133.5 0.7 copy-done.8
  134.3 0.1 copy-done.3
  134.4 2.2 %pass_on.1 = (bf16[128,1280]{1,0:T(8,128)(2,1)}, bf16[128,1280]{1,0:T(8,128)(2,1)}) custom-call(s32[2]{0:T(128)} %pad_add_fusion.place_ref, bf16[128,1280]{1,0:T(8,128)(2,1)} %get-tuple-element.77.four_ref, bf16[128,1280]{1,0:T(8,128)(2,1)} %get-tuple-element.78.two_ref, bf16[128,1280]{1,0:T(8,128)(2,1)} %copy-done.8, bf16[128,1280]{1,0:T(8,128)(2,1)} %copy-done.3), custom_call_target="tpu_custom_call" | custom-call | tf_op jit(solution)/shard_map/pass_on/pallas_call | solution.py:496
  136.6 2.6 %collective-permute-start.15 = (bf16[128,1280]{1,0:T(8,128)(2,1)}, bf16[128,1280]{1,0:T(8,128)(2,1)S(1)}, u32[]{:S(2)}, u32[]{:S(2)}) collective-permute-start(bf16[128,1280]{1,0:T(8,128)(2,1)} %get-tuple-element.80), channel_id=1, source_target_pairs={{2,0},{3,1},{4,2},{5,3},{6,4},{7,5},{8,6},{9,7},{10,8},{11,9},{12,... | collective-permute-start | bytes 983048 | tf_op jit(solution)/shard_map/ppermute | solution.py:721
  139.2 1.9 %collective-permute-start.16 = (bf16[128,1280]{1,0:T(8,128)(2,1)}, bf16[128,1280]{1,0:T(8,128)(2,1)S(1)}, u32[]{:S(2)}, u32[]{:S(2)}) collective-permute-start(bf16[128,1280]{1,0:T(8,128)(2,1)} %get-tuple-element.81), channel_id=1, source_target_pairs={{4,0},{5,1},{6,2},{7,3},{8,4},{9,5},{10,6},{11,7},{12,8},{13,9},{1... | collective-permute-start | bytes 983048 | tf_op jit(solution)/shard_map/ppermute | solution.py:721
  141.2 0.1 reshape.53
  141.3 0.1 copy.25
  141.3 0.7 reshape.54
  142.1 0.1 reshape.55
  142.1 0.1 copy.26
  142.2 0.7 reshape.56
  143.0 0.1 add_add_fusion
  143.0 6.4 %collective-permute-done.15.two_ref = bf16[128,1280]{1,0:T(8,128)(2,1)S(1)} collective-permute-done((bf16[128,1280]{1,0:T(8,128)(2,1)}, bf16[128,1280]{1,0:T(8,128)(2,1)S(1)}, u32[]{:S(2)}, u32[]{:S(2)}) %collective-permute-start.15) | collective-permute-done | bytes 327712 | tf_op jit(solution)/shard_map/ppermute | solution.py:721
  149.4 10.0 %collective-permute-done.16.four_ref = bf16[128,1280]{1,0:T(8,128)(2,1)S(1)} collective-permute-done((bf16[128,1280]{1,0:T(8,128)(2,1)}, bf16[128,1280]{1,0:T(8,128)(2,1)S(1)}, u32[]{:S(2)}, u32[]{:S(2)}) %collective-permute-start.16) | collective-permute-done | bytes 327712 | tf_op jit(solution)/shard_map/ppermute | solution.py:721
  159.4 0.7 slice.10
  160.1 0.6 slice.11
  160.8 1.4 final.1
  (51 shorter events, 0.2 us)
Async XLA Ops:
  0.6 26.7 %copy-start.17 = (f32[1,128,64]{1,2,0:T(8,128)S(1)}, f32[1,128,64]{1,2,0:T(8,128)}, u32[]{:S(2)}) copy-start(f32[1,128,64]{1,2,0:T(8,128)} %param.11) | copy-start | bytes 98308
  2.4 6.0 %collective-permute-start = (bf16[32,1280]{1,0:T(8,128)(2,1)}, bf16[32,1280]{1,0:T(8,128)(2,1)S(1)}, u32[]{:S(2)}, u32[]{:S(2)}) collective-permute-start(bf16[32,1280]{1,0:T(8,128)(2,1)} %get-tuple-element.50), channel_id=1, source_target_pairs={{0,1},{1,2},{2,3},{3,4},{4,5},{5,6},{6,7},{7,8},{8,9},{9,10},{10,1... | collective-permute-start | bytes 245768 | tf_op jit(solution)/shard_map/ppermute | solution.py:721
  8.4 0.6 copy-start.16
  27.3 1.6 %copy-start.7 = (bf16[16,8,1280]{2,1,0:T(8,128)(2,1)}, bf16[16,8,1280]{2,1,0:T(8,128)(2,1)S(1)}, u32[]{:S(2)}) copy-start(bf16[16,8,1280]{2,1,0:T(8,128)(2,1)S(1)} %all_to_all.15) | copy-start | bytes 983044
  27.3 1.6 %collective-permute-start.6 = (bf16[128,1280]{1,0:T(8,128)(2,1)S(1)}, bf16[128,1280]{1,0:T(8,128)(2,1)S(1)}, u32[]{:S(2)}, u32[]{:S(2)}) collective-permute-start(bf16[128,1280]{1,0:T(8,128)(2,1)S(1)} %bitcast.59), channel_id=1, source_target_pairs={{0,1},{1,0},{2,3},{3,2},{4,5},{5,4},{6,7},{7,6},{8,9},{9,8},{10,11... | collective-permute-start | bytes 983048 | tf_op jit(solution)/shard_map/ppermute | solution.py:725
  28.9 0.7 copy-start.22
  29.6 14.5 %copy-start.23 = (bf16[64,1280]{1,0:T(8,128)(2,1)S(1)}, bf16[64,1280]{1,0:T(8,128)(2,1)}, u32[]{:S(2)}) copy-start(bf16[64,1280]{1,0:T(8,128)(2,1)} %get-tuple-element.70) | copy-start | bytes 491524
  43.9 10.9 %copy-start.10 = (bf16[128,1280]{1,0:T(8,128)(2,1)S(1)}, bf16[128,1280]{1,0:T(8,128)(2,1)}, u32[]{:S(2)}) copy-start(bf16[128,1280]{1,0:T(8,128)(2,1)} %get-tuple-element.49.own_ref) | copy-start | bytes 983044
  43.9 38.1 %copy-start.18 = (f32[1,128,64]{1,2,0:T(8,128)S(1)}, f32[1,128,64]{1,2,0:T(8,128)}, u32[]{:S(2)}) copy-start(f32[1,128,64]{1,2,0:T(8,128)} %param.12) | copy-start | bytes 98308
  44.0 2.2 %collective-permute-start.8 = (bf16[128,1280]{1,0:T(8,128)(2,1)}, bf16[128,1280]{1,0:T(8,128)(2,1)S(1)}, u32[]{:S(2)}, u32[]{:S(2)}) collective-permute-start(bf16[128,1280]{1,0:T(8,128)(2,1)} %get-tuple-element.68), channel_id=1, source_target_pairs={{0,1},{1,0},{2,3},{3,2},{4,5},{5,4},{6,7},{7,6},{8,9},{9,8},{10,11... | collective-permute-start | bytes 983048 | tf_op jit(solution)/shard_map/ppermute | solution.py:725
  44.2 1.9 %collective-permute-start.9 = (bf16[64,1280]{1,0:T(8,128)(2,1)S(1)}, bf16[64,1280]{1,0:T(8,128)(2,1)S(1)}, u32[]{:S(2)}, u32[]{:S(2)}) collective-permute-start(bf16[64,1280]{1,0:T(8,128)(2,1)S(1)} %copy-done.23), channel_id=1, source_target_pairs={{0,1},{1,0},{2,3},{3,2},{4,5},{5,4},{6,7},{7,6},{8,9},{9,8},{10,11... | collective-permute-start | bytes 491528 | tf_op jit(solution)/shard_map/ppermute | solution.py:725
  46.1 0.7 copy-start.15
  46.1 0.8 copy-start.9
  49.1 33.7 %all-to-all-start.1 = ((bf16[16,24,1280]{2,1,0:T(8,128)(2,1)}), bf16[16,24,1280]{2,1,0:T(8,128)(2,1)S(1)}, u32[]{:S(2)}, u32[]{:S(2)}) async-start(bf16[16,24,1280]{2,1,0:T(8,128)(2,1)} %fold.1), calls=%async_computation.1 | async-start | bytes 1966080 | tf_op jit(solution)/shard_map/all_to_all | solution.py:731
  54.8 20.8 %collective-permute-start.1 = (bf16[128,1280]{1,0:T(8,128)(2,1)S(1)}, bf16[128,1280]{1,0:T(8,128)(2,1)S(1)}, u32[]{:S(2)}, u32[]{:S(2)}) collective-permute-start(bf16[128,1280]{1,0:T(8,128)(2,1)S(1)} %copy-done.10), channel_id=1, source_target_pairs={{0,4},{1,5},{2,6},{3,7},{4,8},{5,9},{6,10},{7,11},{8,12},{9,13},{1... | collective-permute-start | bytes 983048 | tf_op jit(solution)/shard_map/ppermute | solution.py:721
  58.2 23.8 %collective-permute-start.3 = (bf16[128,1280]{1,0:T(8,128)(2,1)S(1)}, bf16[128,1280]{1,0:T(8,128)(2,1)S(1)}, u32[]{:S(2)}, u32[]{:S(2)}) collective-permute-start(bf16[128,1280]{1,0:T(8,128)(2,1)S(1)} %copy-done.10), channel_id=1, source_target_pairs={{0,2},{1,3},{2,4},{3,5},{4,6},{5,7},{6,8},{7,9},{8,10},{9,11},{10,... | collective-permute-start | bytes 983048 | tf_op jit(solution)/shard_map/ppermute | solution.py:721
  62.1 28.8 %collective-permute-start.5 = (bf16[128,1280]{1,0:T(8,128)(2,1)S(1)}, bf16[128,1280]{1,0:T(8,128)(2,1)S(1)}, u32[]{:S(2)}, u32[]{:S(2)}) collective-permute-start(bf16[128,1280]{1,0:T(8,128)(2,1)S(1)} %copy-done.10), channel_id=1, source_target_pairs={{0,1},{1,0},{2,3},{3,2},{4,5},{5,4},{6,7},{7,6},{8,9},{9,8},{10,11... | collective-permute-start | bytes 983048 | tf_op jit(solution)/shard_map/ppermute | solution.py:725
  75.6 15.4 %copy-start.11 = (bf16[128,1280]{1,0:T(8,128)(2,1)}, bf16[128,1280]{1,0:T(8,128)(2,1)S(1)}, u32[]{:S(2)}) copy-start(bf16[128,1280]{1,0:T(8,128)(2,1)S(1)} %collective-permute-done.1.four) | copy-start | bytes 983044
  75.6 15.3 %collective-permute-start.2 = (bf16[128,1280]{1,0:T(8,128)(2,1)S(1)}, bf16[128,1280]{1,0:T(8,128)(2,1)S(1)}, u32[]{:S(2)}, u32[]{:S(2)}) collective-permute-start(bf16[128,1280]{1,0:T(8,128)(2,1)S(1)} %collective-permute-done.1.four), channel_id=1, source_target_pairs={{0,1},{1,0},{2,3},{3,2},{4,5},{5,4},{6,7},{7,6},{8,9},{9,8},{10,11... | collective-permute-start | bytes 983048 | tf_op jit(solution)/shard_map/ppermute | solution.py:725
  82.0 9.0 %copy-start.12 = (bf16[128,1280]{1,0:T(8,128)(2,1)}, bf16[128,1280]{1,0:T(8,128)(2,1)S(1)}, u32[]{:S(2)}) copy-start(bf16[128,1280]{1,0:T(8,128)(2,1)S(1)} %collective-permute-done.3.two) | copy-start | bytes 983044
  82.0 9.0 %collective-permute-start.4 = (bf16[128,1280]{1,0:T(8,128)(2,1)S(1)}, bf16[128,1280]{1,0:T(8,128)(2,1)}, u32[]{:S(2)}, u32[]{:S(2)}) collective-permute-start(bf16[128,1280]{1,0:T(8,128)(2,1)S(1)} %collective-permute-done.3.two), channel_id=1, source_target_pairs={{0,1},{1,0},{2,3},{3,2},{4,5},{5,4},{6,7},{7,6},{8,9},{9,8},{10,11... | collective-permute-start | bytes 983048 | tf_op jit(solution)/shard_map/ppermute | solution.py:725
  83.7 23.6 %all-to-all-start.2 = ((bf16[16,8,1280]{2,1,0:T(8,128)(2,1)}), bf16[16,8,1280]{2,1,0:T(8,128)(2,1)S(1)}, u32[]{:S(2)}, u32[]{:S(2)}) async-start(bf16[16,8,1280]{2,1,0:T(8,128)(2,1)} %broadcast_in_dim.26), calls=%async_computation.2 | async-start | bytes 655360 | tf_op jit(solution)/shard_map/all_to_all | solution.py:731
  90.9 0.7 copy-start.13
  91.0 0.8 copy-start.14
  107.3 16.7 %collective-permute-start.10 = (bf16[128,1280]{1,0:T(8,128)(2,1)S(1)}, bf16[128,1280]{1,0:T(8,128)(2,1)S(1)}, u32[]{:S(2)}, u32[]{:S(2)}) collective-permute-start(bf16[128,1280]{1,0:T(8,128)(2,1)S(1)} %bitcast.39), channel_id=1, source_target_pairs={{0,1},{1,0},{2,3},{3,2},{4,5},{5,4},{6,7},{7,6},{8,9},{9,8},{10,11... | collective-permute-start | bytes 983048 | tf_op jit(solution)/shard_map/ppermute | solution.py:725
  107.6 16.4 %copy-start = (bf16[6144,192]{0,1:T(8,128)(2,1)S(1)}, bf16[6144,192]{0,1:T(8,128)(2,1)}, u32[]{:S(2)}) copy-start(bf16[6144,192]{0,1:T(8,128)(2,1)} %param.14) | copy-start | bytes 7077892
  107.6 16.4 %copy-start.1 = (bf16[4096,128]{1,0:T(8,128)(2,1)S(1)}, bf16[4096,128]{1,0:T(8,128)(2,1)}, u32[]{:S(2)}) copy-start(bf16[4096,128]{1,0:T(8,128)(2,1)} %wv_ref.3) | copy-start | bytes 3145732
  107.6 16.4 %copy-start.5 = (s32[2]{0:T(128)S(1)}, s32[2]{0:T(128)}, u32[]{:S(2)}) copy-start(s32[2]{0:T(128)} %pad_add_fusion.place_ref) | copy-start | bytes 28
  123.3 10.2 %collective-permute-start.14 = (bf16[128,1280]{1,0:T(8,128)(2,1)}, bf16[128,1280]{1,0:T(8,128)(2,1)S(1)}, u32[]{:S(2)}, u32[]{:S(2)}) collective-permute-start(bf16[128,1280]{1,0:T(8,128)(2,1)} %get-tuple-element.79), channel_id=1, source_target_pairs={{0,1},{1,0},{2,3},{3,2},{4,5},{5,4},{6,7},{7,6},{8,9},{9,8},{10,11... | collective-permute-start | bytes 983048 | tf_op jit(solution)/shard_map/ppermute | solution.py:725
  123.8 17.3 %copy-start.20 = (f32[2,8,256]{2,1,0:T(8,128)S(1)}, f32[2,8,256]{2,1,0:T(8,128)}, u32[]{:S(2)}) copy-start(f32[2,8,256]{2,1,0:T(8,128)} %get-tuple-element.73) | copy-start | bytes 49156
  123.8 17.3 %copy-start.21 = (f32[2,8,256]{2,1,0:T(8,128)S(1)}, f32[2,8,256]{2,1,0:T(8,128)}, u32[]{:S(2)}) copy-start(f32[2,8,256]{2,1,0:T(8,128)} %get-tuple-element.74) | copy-start | bytes 49156
  123.9 17.3 %copy-start.19 = (f32[4,8,256]{2,1,0:T(8,128)S(1)}, f32[4,8,256]{2,1,0:T(8,128)}, u32[]{:S(2)}) copy-start(f32[4,8,256]{2,1,0:T(8,128)} %get-tuple-element.75) | copy-start | bytes 98308
  123.9 9.7 %collective-permute-start.7 = (bf16[128,1280]{1,0:T(8,128)(2,1)}, bf16[128,1280]{1,0:T(8,128)(2,1)S(1)}, u32[]{:S(2)}, u32[]{:S(2)}) collective-permute-start(bf16[128,1280]{1,0:T(8,128)(2,1)} %get-tuple-element.66), channel_id=1, source_target_pairs={{0,1},{1,0},{2,3},{3,2},{4,5},{5,4},{6,7},{7,6},{8,9},{9,8},{10,11... | collective-permute-start | bytes 983048 | tf_op jit(solution)/shard_map/ppermute | solution.py:725
  126.3 34.5 %copy-start.2 = (f32[128,1280]{1,0:T(8,128)S(1)}, f32[128,1280]{1,0:T(8,128)}, u32[]{:S(2)}) copy-start(f32[128,1280]{1,0:T(8,128)} %get-tuple-element.65.keep_ref) | copy-start | bytes 1966084
  126.3 34.5 %copy-start.6 = (s32[2]{0:T(128)S(1)}, s32[2]{0:T(128)}, u32[]{:S(2)}) copy-start(s32[2]{0:T(128)} %pad_add_fusion.place_ref) | copy-start | bytes 28
  126.3 16.6 %collective-permute-start.11 = (bf16[192,384]{1,0:T(8,128)(2,1)S(1)}, bf16[192,384]{1,0:T(8,128)(2,1)S(1)}, u32[]{:S(2)}, u32[]{:S(2)}) collective-permute-start(bf16[192,384]{1,0:T(8,128)(2,1)S(1)} %get-tuple-element.71), channel_id=1, source_target_pairs={{0,64},{32,96},{64,0},{96,32},{1,65},{33,97},{65,1},{97,33},{2,66}... | collective-permute-start | bytes 442376 | tf_op jit(solution)/shard_map/ppermute | solution.py:721
  130.3 12.7 %collective-permute-start.12 = (bf16[192,384]{1,0:T(8,128)(2,1)S(1)}, bf16[192,384]{1,0:T(8,128)(2,1)S(1)}, u32[]{:S(2)}, u32[]{:S(2)}) collective-permute-start(bf16[192,384]{1,0:T(8,128)(2,1)S(1)} %get-tuple-element.71), channel_id=1, source_target_pairs={{0,32},{32,64},{64,96},{96,0},{1,33},{33,65},{65,97},{97,1},{2,34}... | collective-permute-start | bytes 442376 | tf_op jit(solution)/shard_map/ppermute | solution.py:721
  131.3 11.6 %collective-permute-start.13 = (bf16[192,384]{1,0:T(8,128)(2,1)S(1)}, bf16[192,384]{1,0:T(8,128)(2,1)S(1)}, u32[]{:S(2)}, u32[]{:S(2)}) collective-permute-start(bf16[192,384]{1,0:T(8,128)(2,1)S(1)} %get-tuple-element.71), channel_id=1, source_target_pairs={{0,96},{32,0},{64,32},{96,64},{1,97},{33,1},{65,33},{97,65},{2,98}... | collective-permute-start | bytes 442376 | tf_op jit(solution)/shard_map/ppermute | solution.py:721
  133.5 0.7 copy-start.8
  133.5 0.9 copy-start.3
  136.6 24.2 %copy-start.4 = (bf16[128,1280]{1,0:T(8,128)(2,1)S(1)}, bf16[128,1280]{1,0:T(8,128)(2,1)}, u32[]{:S(2)}) copy-start(bf16[128,1280]{1,0:T(8,128)(2,1)} %copy-done.3) | copy-start | bytes 983044
  136.6 12.8 %collective-permute-start.15 = (bf16[128,1280]{1,0:T(8,128)(2,1)}, bf16[128,1280]{1,0:T(8,128)(2,1)S(1)}, u32[]{:S(2)}, u32[]{:S(2)}) collective-permute-start(bf16[128,1280]{1,0:T(8,128)(2,1)} %get-tuple-element.80), channel_id=1, source_target_pairs={{2,0},{3,1},{4,2},{5,3},{6,4},{7,5},{8,6},{9,7},{10,8},{11,9},{12,... | collective-permute-start | bytes 983048 | tf_op jit(solution)/shard_map/ppermute | solution.py:721
  139.2 20.2 %collective-permute-start.16 = (bf16[128,1280]{1,0:T(8,128)(2,1)}, bf16[128,1280]{1,0:T(8,128)(2,1)S(1)}, u32[]{:S(2)}, u32[]{:S(2)}) collective-permute-start(bf16[128,1280]{1,0:T(8,128)(2,1)} %get-tuple-element.81), channel_id=1, source_target_pairs={{4,0},{5,1},{6,2},{7,3},{8,4},{9,5},{10,6},{11,7},{12,8},{13,9},{1... | collective-permute-start | bytes 983048 | tf_op jit(solution)/shard_map/ppermute | solution.py:721
